TPU v7x, 256 devices: a whole 4x4x8 slice. The times are simulated.
256 devices in a mesh: sector: 16 (over y, x_hi, core), depth: 16 (over x_lo, z).
Axes of the slice: x: 4 (x_hi: 2, x_lo: 2; x = x_hi * 2 + x_lo), y: 4, z: 8, core: 2. Of those that a mesh axis runs over, the one named last changes fastest.
Arguments:
- panel: bfloat16 [1048576, 128], P(('sector', 'depth')), may hold values from -6 to 6
- coords: int32 [3, 1048576], P(None, ('sector', 'depth')), may hold values from 0 to 127, as said below
- neighbours: int32 [8192, 32], P(('sector', 'depth')), may hold values from 0 to 8191, as said below
- ranges: float32 [3], replicated, may hold values from 6 to 20
Outputs:
- basis: float32 [1048576, 128], P(('sector', 'depth'))
- factor: float32 [128, 128], replicated
Inputs may be any that keep to these rules, and one draw needn't show every extreme that they name: `coords`: each device's 32 * 128 cells occupy every point of its own grid box exactly once: azimuth columns s * 8 to (s + 1) * 8 - 1 for sector s, radial rows 0 to 63, depth layers d * 8 to (d + 1) * 8 - 1 for slab d, in an arbitrary order; cell blocks are numbered sector-major, then slab, then block. `neighbours`: each row lists 32 different block columns, all of the row's depth slab and of sectors at most two away from its own around the cycle.
All inputs are finite; a program needn't handle non-finite values.
Results may differ from a plain program's by a relative error of at most 0.0065.
Values may be sent and summed in bfloat16 or wider, within the bound.
A program may use at most 128 MiB of HBM per device.

v0:
```python
import jax
import jax.numpy as jnp
from jax import lax
from jax.sharding import PartitionSpec as P

AZ_SEC = 8


CUTOFF = 3.0
NUGGET = 0.5


def passed_along(block, axis, distance):
    devices = range(lax.axis_size(axis))
    route = [((i - distance) % len(devices), i) for i in devices]
    return lax.ppermute(block, axis, route)


def as_sent(value):

    def short(part):
        return part.astype(jnp.bfloat16) if part.dtype == jnp.float32 else part

    return jax.tree.map(short, value)


def cov_blocks(home, remote, ranges, period):
    diffs = (home[:, None, :, :, None] - remote[:, :, :, None, :]).astype(jnp.float32)
    along = jnp.abs(diffs[:, :, 0])
    along = jnp.minimum(along, period - along)
    scaled = (
        (along / ranges[0]) ** 2
        + (diffs[:, :, 1] / ranges[1]) ** 2
        + (diffs[:, :, 2] / ranges[2]) ** 2
    )
    radius = jnp.sqrt(scaled)
    taper = jnp.maximum(1.0 - radius / CUTOFF, 0.0)
    weight = 8.0 / jnp.sqrt(jnp.float32(remote.shape[1] * remote.shape[3]))
    return (weight * jnp.exp(-radius) * taper * taper).astype(jnp.bfloat16)


def on_device(panel, coords, neighbours, ranges):
    block_count = neighbours.shape[0]
    block_size = panel.shape[0] // block_count
    width = panel.shape[1]
    sector_count = lax.axis_size("sector")
    slab_count = lax.axis_size("depth")
    my_sector = lax.axis_index("sector")
    blocked = panel.reshape(block_count, block_size, width)
    near_side = {}
    far_side = {}
    for direction in (1, -1):
        near_side[direction] = passed_along((blocked, coords), "sector", direction)
    for direction in (1, -1):
        far_side[direction] = passed_along(
            (near_side[direction][0], as_sent(near_side[direction][1])), "sector", direction
        )
    ordered = [far_side[1], near_side[1], (blocked, coords), near_side[-1], far_side[-1]]
    wide_panel = jnp.concatenate([member[0] for member in ordered], axis=0)
    wide_coords = jnp.concatenate(
        [member[1].reshape(3, block_count, block_size) for member in ordered], axis=1
    )
    wide_coords = jnp.transpose(wide_coords, (1, 0, 2))
    home_coords = jnp.transpose(coords.reshape(3, block_count, block_size), (1, 0, 2))
    column_sector = neighbours // (slab_count * block_count)
    step_away = (column_sector - my_sector + 2) % sector_count
    local_column = step_away * block_count + neighbours % block_count
    period = jnp.float32(AZ_SEC * sector_count)
    group = 4
    turns = block_count // group

    def one_group(inputs):
        rows_coords, rows_panel, rows_list = inputs
        kernel = cov_blocks(rows_coords, wide_coords[rows_list], ranges, period)
        product = jnp.einsum(
            "gnab,gnbc->gac", kernel, wide_panel[rows_list], preferred_element_type=jnp.float32
        )
        return product + NUGGET * rows_panel.astype(jnp.float32)

    image = lax.map(
        one_group,
        (
            home_coords.reshape(turns, group, 3, block_size),
            blocked.reshape(turns, group, block_size, width),
            local_column.reshape(turns, group, -1),
        ),
    )
    image = image.reshape(block_count * block_size, width)
    total_cells = jnp.float32(image.shape[0] * sector_count * slab_count)
    local_gram = (
        jnp.dot(image.T, image, precision=lax.Precision.HIGHEST, preferred_element_type=jnp.float32)
        / total_cells
    )
    lower = jnp.linalg.cholesky(lax.psum(local_gram, ("sector", "depth")))
    inverse = jax.scipy.linalg.solve_triangular(
        lower, jnp.eye(width, dtype=jnp.float32), lower=True
    )
    basis = jnp.dot(
        image, inverse.T, precision=lax.Precision.HIGHEST, preferred_element_type=jnp.float32
    )
    return (basis, lower.T)


def solution(mesh):
    in_specs = (
        P(("sector", "depth"), None),
        P(None, ("sector", "depth")),
        P(("sector", "depth"), None),
        P(),
    )
    out_specs = (P(("sector", "depth"), None), P())
    return jax.shard_map(
        on_device, mesh=mesh, in_specs=in_specs, out_specs=out_specs, check_vma=False
    )
```

profile of v0, /device:TPU:1, one launch (start us, length us, event | category | flops | bytes accessed | tf_op | source)
XLA Modules:
  0.0 625.7 jit_solution(4741672495982144289)
XLA Ops:
  7.2 4.2 collective-permute-start.4
  11.4 3.2 collective-permute-start
  14.7 1.2 collective-permute-start.2
  15.9 15.5 %collective-permute-done = s32[3,4096]{1,0:T(4,128)S(1)} collective-permute-done((s32[3,4096]{1,0:T(4,128)}, s32[3,4096]{1,0:T(4,128)S(1)}, u32[]{:S(2)}, u32[]{:S(2)}) %collective-permute-start) | collective-permute-done | bytes 49184 | tf_op jit(solution)/shard_map/ppermute | solution.py:16
  31.4 3.9 collective-permute-start.1
  36.0 1.9 collective-permute-done.2
  38.0 2.1 collective-permute-start.3
  40.1 1.2 collective-permute-start.5
  41.3 5.5 collective-permute-start.7
  46.8 0.8 constant_dynamic-update-slice_fusion
  47.9 8.0 %collective-permute-done.5 = bf16[32,128,128]{2,1,0:T(8,128)(2,1)S(1)} collective-permute-done((bf16[32,128,128]{2,1,0:T(8,128)(2,1)}, bf16[32,128,128]{2,1,0:T(8,128)(2,1)S(1)}, u32[]{:S(2)}, u32[]{:S(2)}) %collective-permute-start.5) | collective-permute-done | bytes 1048608 | tf_op jit(solution)/shard_map/ppermute | solution.py:16
  56.0 1.4 constant_dynamic-update-slice_fusion.4
  57.5 1.4 constant_dynamic-update-slice_fusion.2
  59.0 9.7 %collective-permute-done.7 = bf16[32,128,128]{2,1,0:T(8,128)(2,1)S(1)} collective-permute-done((bf16[32,128,128]{2,1,0:T(8,128)(2,1)}, bf16[32,128,128]{2,1,0:T(8,128)(2,1)S(1)}, u32[]{:S(2)}, u32[]{:S(2)}) %collective-permute-start.7) | collective-permute-done | bytes 1048608 | tf_op jit(solution)/shard_map/ppermute | solution.py:16
  68.8 2.4 copy-done
  71.2 272.4 %while.10 = (s32[]{:T(128)}, f32[8,4,128,128]{3,2,1,0:T(8,128)S(1)}, s32[8,4,3,128]{3,1,0,2:T(4,128)S(1)}, s32[8,4,32]{2,1,0:T(4,128)S(1)}, s32[160,3,128]{2,1,0...) while((s32[]{:T(128)}, ...), condition=%wide.region_1.2_spmd, body=%wide.region_0.1_spmd.sunk | while | flops 589497728 | bytes 68511408 | solution.py:80
  72.1 11.8 %subtract_convert_fusion.2 = f32[4,32,3,128,128]{4,3,1,0,2:T(8,128)} fusion(s32[4,32,3,128]{3,1,0,2:T(8,128)S(1)} %copy.35, s32[4,3,128]{2,0,1:T(4,128)S(1)} %dynamic-slice_bitcast_fusion.2), kind=kLoop, calls=%fused_computation.2.clone.1 | loop fusion | flops 12582912 | bytes 25368576 | tf_op jit(solution)/shard_map/while/body/eval_jaxpr/convert_element_type | solution.py:28
  84.0 5.6 gather_fusion
  90.2 15.0 %fusion.56 = f32[8,4,128,128]{3,2,1,0:T(8,128)S(1)} fusion(f32[8,4,128,128]{3,2,1,0:T(8,128)S(1)} %get-tuple-element.145, s32[]{:T(128)} %get-tuple-element.144, bf16[4,32,128,128]{3,2,1,0:T(8,128)(2,1)} %bitcast.145, f32[4,32,3,128,128]{4,3,1,0,2:T(8,128)} %subtract_convert_fusion.2, f32[]{:T(128)} %bitcast.142, f32[]{:T(128)} %bitcast.143, ...), kind=kOutput, calls=%fused_computation.23.clone.1 | convolution fusion | flops 576913408 | bytes 29753360 | tf_op jit(solution)/shard_map/while/body/eval_jaxpr/gnab,gnbc->gac/dot_general | solution.py:75
  106.2 11.8 %subtract_convert_fusion.2 = f32[4,32,3,128,128]{4,3,1,0,2:T(8,128)} fusion(s32[4,32,3,128]{3,1,0,2:T(8,128)S(1)} %copy.35, s32[4,3,128]{2,0,1:T(4,128)S(1)} %dynamic-slice_bitcast_fusion.2), kind=kLoop, calls=%fused_computation.2.clone.1 | loop fusion | flops 12582912 | bytes 25368576 | tf_op jit(solution)/shard_map/while/body/eval_jaxpr/convert_element_type | solution.py:28
  118.0 5.6 gather_fusion
  124.2 15.0 %fusion.56 = f32[8,4,128,128]{3,2,1,0:T(8,128)S(1)} fusion(f32[8,4,128,128]{3,2,1,0:T(8,128)S(1)} %get-tuple-element.145, s32[]{:T(128)} %get-tuple-element.144, bf16[4,32,128,128]{3,2,1,0:T(8,128)(2,1)} %bitcast.145, f32[4,32,3,128,128]{4,3,1,0,2:T(8,128)} %subtract_convert_fusion.2, f32[]{:T(128)} %bitcast.142, f32[]{:T(128)} %bitcast.143, ...), kind=kOutput, calls=%fused_computation.23.clone.1 | convolution fusion | flops 576913408 | bytes 29753360 | tf_op jit(solution)/shard_map/while/body/eval_jaxpr/gnab,gnbc->gac/dot_general | solution.py:75
  140.2 11.8 %subtract_convert_fusion.2 = f32[4,32,3,128,128]{4,3,1,0,2:T(8,128)} fusion(s32[4,32,3,128]{3,1,0,2:T(8,128)S(1)} %copy.35, s32[4,3,128]{2,0,1:T(4,128)S(1)} %dynamic-slice_bitcast_fusion.2), kind=kLoop, calls=%fused_computation.2.clone.1 | loop fusion | flops 12582912 | bytes 25368576 | tf_op jit(solution)/shard_map/while/body/eval_jaxpr/convert_element_type | solution.py:28
  152.0 5.6 gather_fusion
  158.3 15.0 %fusion.56 = f32[8,4,128,128]{3,2,1,0:T(8,128)S(1)} fusion(f32[8,4,128,128]{3,2,1,0:T(8,128)S(1)} %get-tuple-element.145, s32[]{:T(128)} %get-tuple-element.144, bf16[4,32,128,128]{3,2,1,0:T(8,128)(2,1)} %bitcast.145, f32[4,32,3,128,128]{4,3,1,0,2:T(8,128)} %subtract_convert_fusion.2, f32[]{:T(128)} %bitcast.142, f32[]{:T(128)} %bitcast.143, ...), kind=kOutput, calls=%fused_computation.23.clone.1 | convolution fusion | flops 576913408 | bytes 29753360 | tf_op jit(solution)/shard_map/while/body/eval_jaxpr/gnab,gnbc->gac/dot_general | solution.py:75
  173.4 0.8 gather_fusion.1
  174.2 11.8 %subtract_convert_fusion.2 = f32[4,32,3,128,128]{4,3,1,0,2:T(8,128)} fusion(s32[4,32,3,128]{3,1,0,2:T(8,128)S(1)} %copy.35, s32[4,3,128]{2,0,1:T(4,128)S(1)} %dynamic-slice_bitcast_fusion.2), kind=kLoop, calls=%fused_computation.2.clone.1 | loop fusion | flops 12582912 | bytes 25368576 | tf_op jit(solution)/shard_map/while/body/eval_jaxpr/convert_element_type | solution.py:28
  186.0 5.6 gather_fusion
  192.3 15.0 %fusion.56 = f32[8,4,128,128]{3,2,1,0:T(8,128)S(1)} fusion(f32[8,4,128,128]{3,2,1,0:T(8,128)S(1)} %get-tuple-element.145, s32[]{:T(128)} %get-tuple-element.144, bf16[4,32,128,128]{3,2,1,0:T(8,128)(2,1)} %bitcast.145, f32[4,32,3,128,128]{4,3,1,0,2:T(8,128)} %subtract_convert_fusion.2, f32[]{:T(128)} %bitcast.142, f32[]{:T(128)} %bitcast.143, ...), kind=kOutput, calls=%fused_computation.23.clone.1 | convolution fusion | flops 576913408 | bytes 29753360 | tf_op jit(solution)/shard_map/while/body/eval_jaxpr/gnab,gnbc->gac/dot_general | solution.py:75
  208.2 11.8 %subtract_convert_fusion.2 = f32[4,32,3,128,128]{4,3,1,0,2:T(8,128)} fusion(s32[4,32,3,128]{3,1,0,2:T(8,128)S(1)} %copy.35, s32[4,3,128]{2,0,1:T(4,128)S(1)} %dynamic-slice_bitcast_fusion.2), kind=kLoop, calls=%fused_computation.2.clone.1 | loop fusion | flops 12582912 | bytes 25368576 | tf_op jit(solution)/shard_map/while/body/eval_jaxpr/convert_element_type | solution.py:28
  220.1 5.6 gather_fusion
  226.3 15.0 %fusion.56 = f32[8,4,128,128]{3,2,1,0:T(8,128)S(1)} fusion(f32[8,4,128,128]{3,2,1,0:T(8,128)S(1)} %get-tuple-element.145, s32[]{:T(128)} %get-tuple-element.144, bf16[4,32,128,128]{3,2,1,0:T(8,128)(2,1)} %bitcast.145, f32[4,32,3,128,128]{4,3,1,0,2:T(8,128)} %subtract_convert_fusion.2, f32[]{:T(128)} %bitcast.142, f32[]{:T(128)} %bitcast.143, ...), kind=kOutput, calls=%fused_computation.23.clone.1 | convolution fusion | flops 576913408 | bytes 29753360 | tf_op jit(solution)/shard_map/while/body/eval_jaxpr/gnab,gnbc->gac/dot_general | solution.py:75
  242.3 11.8 %subtract_convert_fusion.2 = f32[4,32,3,128,128]{4,3,1,0,2:T(8,128)} fusion(s32[4,32,3,128]{3,1,0,2:T(8,128)S(1)} %copy.35, s32[4,3,128]{2,0,1:T(4,128)S(1)} %dynamic-slice_bitcast_fusion.2), kind=kLoop, calls=%fused_computation.2.clone.1 | loop fusion | flops 12582912 | bytes 25368576 | tf_op jit(solution)/shard_map/while/body/eval_jaxpr/convert_element_type | solution.py:28
  254.1 5.6 gather_fusion
  260.3 15.0 %fusion.56 = f32[8,4,128,128]{3,2,1,0:T(8,128)S(1)} fusion(f32[8,4,128,128]{3,2,1,0:T(8,128)S(1)} %get-tuple-element.145, s32[]{:T(128)} %get-tuple-element.144, bf16[4,32,128,128]{3,2,1,0:T(8,128)(2,1)} %bitcast.145, f32[4,32,3,128,128]{4,3,1,0,2:T(8,128)} %subtract_convert_fusion.2, f32[]{:T(128)} %bitcast.142, f32[]{:T(128)} %bitcast.143, ...), kind=kOutput, calls=%fused_computation.23.clone.1 | convolution fusion | flops 576913408 | bytes 29753360 | tf_op jit(solution)/shard_map/while/body/eval_jaxpr/gnab,gnbc->gac/dot_general | solution.py:75
  276.3 11.8 %subtract_convert_fusion.2 = f32[4,32,3,128,128]{4,3,1,0,2:T(8,128)} fusion(s32[4,32,3,128]{3,1,0,2:T(8,128)S(1)} %copy.35, s32[4,3,128]{2,0,1:T(4,128)S(1)} %dynamic-slice_bitcast_fusion.2), kind=kLoop, calls=%fused_computation.2.clone.1 | loop fusion | flops 12582912 | bytes 25368576 | tf_op jit(solution)/shard_map/while/body/eval_jaxpr/convert_element_type | solution.py:28
  288.1 5.6 gather_fusion
  294.4 15.0 %fusion.56 = f32[8,4,128,128]{3,2,1,0:T(8,128)S(1)} fusion(f32[8,4,128,128]{3,2,1,0:T(8,128)S(1)} %get-tuple-element.145, s32[]{:T(128)} %get-tuple-element.144, bf16[4,32,128,128]{3,2,1,0:T(8,128)(2,1)} %bitcast.145, f32[4,32,3,128,128]{4,3,1,0,2:T(8,128)} %subtract_convert_fusion.2, f32[]{:T(128)} %bitcast.142, f32[]{:T(128)} %bitcast.143, ...), kind=kOutput, calls=%fused_computation.23.clone.1 | convolution fusion | flops 576913408 | bytes 29753360 | tf_op jit(solution)/shard_map/while/body/eval_jaxpr/gnab,gnbc->gac/dot_general | solution.py:75
  310.3 11.8 %subtract_convert_fusion.2 = f32[4,32,3,128,128]{4,3,1,0,2:T(8,128)} fusion(s32[4,32,3,128]{3,1,0,2:T(8,128)S(1)} %copy.35, s32[4,3,128]{2,0,1:T(4,128)S(1)} %dynamic-slice_bitcast_fusion.2), kind=kLoop, calls=%fused_computation.2.clone.1 | loop fusion | flops 12582912 | bytes 25368576 | tf_op jit(solution)/shard_map/while/body/eval_jaxpr/convert_element_type | solution.py:28
  322.1 5.6 gather_fusion
  328.4 15.0 %fusion.56 = f32[8,4,128,128]{3,2,1,0:T(8,128)S(1)} fusion(f32[8,4,128,128]{3,2,1,0:T(8,128)S(1)} %get-tuple-element.145, s32[]{:T(128)} %get-tuple-element.144, bf16[4,32,128,128]{3,2,1,0:T(8,128)(2,1)} %bitcast.145, f32[4,32,3,128,128]{4,3,1,0,2:T(8,128)} %subtract_convert_fusion.2, f32[]{:T(128)} %bitcast.142, f32[]{:T(128)} %bitcast.143, ...), kind=kOutput, calls=%fused_computation.23.clone.1 | convolution fusion | flops 576913408 | bytes 29753360 | tf_op jit(solution)/shard_map/while/body/eval_jaxpr/gnab,gnbc->gac/dot_general | solution.py:75
  343.6 4.1 fusion.30
  347.8 242.3 %all-reduce.2.cloned.1.call-done = f32[128,128]{0,1:T(8,128)} async-done(((f32[128,128]{0,1:T(8,128)}), f32[128,128]{0,1:T(8,128)}) %all-reduce.2.cloned.1.call-update) | async-done | bytes 65552 | tf_op jit(solution)/shard_map/psum | solution.py:94
  590.1 0.9 copy.16
  591.0 0.9 fusion.33
  591.9 11.7 %cholesky.17 = f32[128,128]{1,0:T(8,128)S(1)} custom-call(f32[128,128]{1,0:T(8,128)S(1)} %fusion.33), custom_call_target="Cholesky" | custom-call | tf_op jit(solution)/shard_map/jit(cholesky)/cholesky | solution.py:94
  604.9 9.8 %custom-call.7 = f32[1,128,128]{1,2,0:T(8,128)S(1)} custom-call(f32[1,128,128]{2,1,0:T(8,128)S(1)} %get-tuple-element.79), custom_call_target="InvertDiagBlocksLowerTriangular" | custom-call | tf_op jit(solution)/shard_map/jit(_solve_triangular)/triangular_solve | solution.py:95
  615.7 3.1 fusion.43
  (98 shorter events, 15.3 us)
Async XLA Ops:
  7.2 50.2 %copy-start.1 = (bf16[4096,128]{1,0:T(8,128)(2,1)S(1)}, bf16[4096,128]{1,0:T(8,128)(2,1)}, u32[]{:S(2)}) copy-start(bf16[4096,128]{1,0:T(8,128)(2,1)} %param.6) | copy-start | bytes 3145732
  7.2 582.9 %all-reduce.2.cloned.1.call-start = ((), (), s32[]{:S(2)}) async-start(), calls=%async_computation | async-start | bytes 131072 | tf_op jit(solution)/shard_map/psum | solution.py:94
  7.2 32.9 %collective-permute-start.4 = (bf16[32,128,128]{2,1,0:T(8,128)(2,1)}, bf16[32,128,128]{2,1,0:T(8,128)(2,1)}, u32[]{:S(2)}, u32[]{:S(2)}) collective-permute-start(bf16[32,128,128]{2,1,0:T(8,128)(2,1)} %bitcast.148), channel_id=1, source_target_pairs={{240,0},{0,16},{16,32},{32,48},{48,64},{64,80},{80,96},{96,112},{1... | collective-permute-start | bytes 3145736 | tf_op jit(solution)/shard_map/ppermute | solution.py:16
  11.4 29.8 %collective-permute-start.6 = (bf16[32,128,128]{2,1,0:T(8,128)(2,1)}, bf16[32,128,128]{2,1,0:T(8,128)(2,1)}, u32[]{:S(2)}, u32[]{:S(2)}) collective-permute-start(bf16[32,128,128]{2,1,0:T(8,128)(2,1)} %bitcast.149), channel_id=1, source_target_pairs={{16,0},{32,16},{48,32},{64,48},{80,64},{96,80},{112,96},{128,112},... | collective-permute-start | bytes 3145736 | tf_op jit(solution)/shard_map/ppermute | solution.py:16
  11.4 20.0 %collective-permute-start = (s32[3,4096]{1,0:T(4,128)}, s32[3,4096]{1,0:T(4,128)S(1)}, u32[]{:S(2)}, u32[]{:S(2)}) collective-permute-start(s32[3,4096]{1,0:T(4,128)} %param.7), channel_id=1, source_target_pairs={{240,0},{0,16},{16,32},{32,48},{48,64},{64,80},{80,96},{96,112},{1... | collective-permute-start | bytes 147464 | tf_op jit(solution)/shard_map/ppermute | solution.py:16
  14.7 23.3 %collective-permute-start.2 = (s32[3,4096]{1,0:T(4,128)}, s32[3,4096]{1,0:T(4,128)S(1)}, u32[]{:S(2)}, u32[]{:S(2)}) collective-permute-start(s32[3,4096]{1,0:T(4,128)} %param.7), channel_id=1, source_target_pairs={{16,0},{32,16},{48,32},{64,48},{80,64},{96,80},{112,96},{128,112},... | collective-permute-start | bytes 147464 | tf_op jit(solution)/shard_map/ppermute | solution.py:16
  31.4 9.8 %collective-permute-start.1 = (s32[3,4096]{1,0:T(4,128)S(1)}, s32[3,4096]{1,0:T(4,128)S(1)}, u32[]{:S(2)}, u32[]{:S(2)}) collective-permute-start(s32[3,4096]{1,0:T(4,128)S(1)} %collective-permute-done), channel_id=1, source_target_pairs={{240,0},{0,16},{16,32},{32,48},{48,64},{64,80},{80,96},{96,112},{1... | collective-permute-start | bytes 147464 | tf_op jit(solution)/shard_map/ppermute | solution.py:16
  38.0 9.7 %collective-permute-start.3 = (s32[3,4096]{1,0:T(4,128)S(1)}, s32[3,4096]{1,0:T(4,128)S(1)}, u32[]{:S(2)}, u32[]{:S(2)}) collective-permute-start(s32[3,4096]{1,0:T(4,128)S(1)} %collective-permute-done.2), channel_id=1, source_target_pairs={{16,0},{32,16},{48,32},{64,48},{80,64},{96,80},{112,96},{128,112},... | collective-permute-start | bytes 147464 | tf_op jit(solution)/shard_map/ppermute | solution.py:16
  40.1 15.8 %collective-permute-start.5 = (bf16[32,128,128]{2,1,0:T(8,128)(2,1)}, bf16[32,128,128]{2,1,0:T(8,128)(2,1)S(1)}, u32[]{:S(2)}, u32[]{:S(2)}) collective-permute-start(bf16[32,128,128]{2,1,0:T(8,128)(2,1)} %collective-permute-done.4), channel_id=1, source_target_pairs={{240,0},{0,16},{16,32},{32,48},{48,64},{64,80},{80,96},{96,112},{1... | collective-permute-start | bytes 3145736 | tf_op jit(solution)/shard_map/ppermute | solution.py:16
  41.3 27.4 %collective-permute-start.7 = (bf16[32,128,128]{2,1,0:T(8,128)(2,1)}, bf16[32,128,128]{2,1,0:T(8,128)(2,1)S(1)}, u32[]{:S(2)}, u32[]{:S(2)}) collective-permute-start(bf16[32,128,128]{2,1,0:T(8,128)(2,1)} %collective-permute-done.6), channel_id=1, source_target_pairs={{16,0},{32,16},{48,32},{64,48},{80,64},{96,80},{112,96},{128,112},... | collective-permute-start | bytes 3145736 | tf_op jit(solution)/shard_map/ppermute | solution.py:16
  47.9 23.4 %copy-start.3 = (f32[3]{0:T(128)S(1)}, f32[3]{0:T(128)}, u32[]{:S(2)}) copy-start(f32[3]{0:T(128)} %param.9) | copy-start | bytes 40
  68.8 2.4 copy-start
  84.0 6.3 %copy-start.2 = (bf16[4096,128]{1,0:T(8,128)(2,1)S(1)}, bf16[4096,128]{1,0:T(8,128)(2,1)}, u32[]{:S(2)}) copy-start(bf16[4096,128]{1,0:T(8,128)(2,1)} %get-tuple-element.174) | copy-start | bytes 3145732 | tf_op jit(solution)/shard_map/while
  118.0 6.3 %copy-start.2 = (bf16[4096,128]{1,0:T(8,128)(2,1)S(1)}, bf16[4096,128]{1,0:T(8,128)(2,1)}, u32[]{:S(2)}) copy-start(bf16[4096,128]{1,0:T(8,128)(2,1)} %get-tuple-element.174) | copy-start | bytes 3145732 | tf_op jit(solution)/shard_map/while
  152.0 6.3 %copy-start.2 = (bf16[4096,128]{1,0:T(8,128)(2,1)S(1)}, bf16[4096,128]{1,0:T(8,128)(2,1)}, u32[]{:S(2)}) copy-start(bf16[4096,128]{1,0:T(8,128)(2,1)} %get-tuple-element.174) | copy-start | bytes 3145732 | tf_op jit(solution)/shard_map/while
  186.0 6.3 %copy-start.2 = (bf16[4096,128]{1,0:T(8,128)(2,1)S(1)}, bf16[4096,128]{1,0:T(8,128)(2,1)}, u32[]{:S(2)}) copy-start(bf16[4096,128]{1,0:T(8,128)(2,1)} %get-tuple-element.174) | copy-start | bytes 3145732 | tf_op jit(solution)/shard_map/while
  220.1 6.3 %copy-start.2 = (bf16[4096,128]{1,0:T(8,128)(2,1)S(1)}, bf16[4096,128]{1,0:T(8,128)(2,1)}, u32[]{:S(2)}) copy-start(bf16[4096,128]{1,0:T(8,128)(2,1)} %get-tuple-element.174) | copy-start | bytes 3145732 | tf_op jit(solution)/shard_map/while
  254.1 6.3 %copy-start.2 = (bf16[4096,128]{1,0:T(8,128)(2,1)S(1)}, bf16[4096,128]{1,0:T(8,128)(2,1)}, u32[]{:S(2)}) copy-start(bf16[4096,128]{1,0:T(8,128)(2,1)} %get-tuple-element.174) | copy-start | bytes 3145732 | tf_op jit(solution)/shard_map/while
  288.1 6.3 %copy-start.2 = (bf16[4096,128]{1,0:T(8,128)(2,1)S(1)}, bf16[4096,128]{1,0:T(8,128)(2,1)}, u32[]{:S(2)}) copy-start(bf16[4096,128]{1,0:T(8,128)(2,1)} %get-tuple-element.174) | copy-start | bytes 3145732 | tf_op jit(solution)/shard_map/while
  322.1 6.3 %copy-start.2 = (bf16[4096,128]{1,0:T(8,128)(2,1)S(1)}, bf16[4096,128]{1,0:T(8,128)(2,1)}, u32[]{:S(2)}) copy-start(bf16[4096,128]{1,0:T(8,128)(2,1)} %get-tuple-element.174) | copy-start | bytes 3145732 | tf_op jit(solution)/shard_map/while
Sparse Core Ops, SparseCore 0:
  347.9 242.1 all-reduce.1
where the time goes:
time: 626 us
  waiting for transfers between devices  278 us (44%)
  matrix products  128 us (20%)
  other arithmetic  119 us (19%)
  local copies, waits for them, and re-layouts  65.2 us (10%)
  starting transfers between devices  21.4 us (3%)
  between operations  14.2 us (2%)
    psum x1, waiting for transfers between devices, on_device(): lower = jnp.linalg.cholesky(lax.psum(local_gram, ('sector', 'depth')))  242 us
    dot_general x8, matrix products, one_group(): jnp.einsum('gnab,gnbc->gac', kernel, wide_panel[rows_list], preferred_ele...  120 us
    convert_element_type x8, other arithmetic, cov_blocks(): (home[:, None, :, :, None] - remote[:, :, :, None, :]).astype(jnp.float32)  94.5 us
    gather x8, local copies, waits for them, and re-layouts, one_group(): wide_panel[rows_list]  44.8 us
    ppermute x8, waiting for transfers between devices, passed_along(): return lax.ppermute(block, axis, route)  35.2 us
    ppermute x8, starting transfers between devices, passed_along(): return lax.ppermute(block, axis, route)  21.3 us
  transfers between devices with their start and end apart: 9, of which 5 were waited for; matrix products, arithmetic and copies ran while one was open for 1% of the time, Pallas kernels for 0%

commit v1 on v0

v1 whole, which is shorter than its diff:
```python
import functools

import jax
import jax.numpy as jnp
from jax import lax
from jax.experimental import pallas as pl
from jax.experimental.pallas import tpu as pltpu
from jax.sharding import PartitionSpec as P

AZ_SEC = 8
DZ = 8
CUTOFF = 3.0
NUGGET = 0.5
BS = 128
LOG2E = 1.4426950408889634
MESH = pl.DeviceIdType.MESH
F32 = jnp.float32
BF16 = jnp.bfloat16
HIGHEST = lax.Precision.HIGHEST


def passed_along(block, axis, distance):
    devices = range(lax.axis_size(axis))
    route = [((i - distance) % len(devices), i) for i in devices]
    return lax.ppermute(block, axis, route)


def pieces(value):
    one = lax.reduce_precision(value, 8, 7)
    two = lax.reduce_precision(value - one, 8, 7)
    three = value - one - two
    return one, two, three


def image_kernel(cols, left_ref, right_ref, panel_ref, own_ref, image_ref, gram_ref):
    rows = left_ref.shape[0]
    slots = cols.shape[1]
    rank = panel_ref.shape[2]
    gram_ref[...] = jnp.zeros_like(gram_ref)

    def one_row(g, carry):
        left = left_ref[g]
        acc = jnp.zeros((BS, rank), F32)
        for n in range(0, slots, 2):
            ha = cols[g, n]
            hb = cols[g, n + 1]
            right = jnp.concatenate([right_ref[ha], right_ref[hb]], axis=1)
            square = jnp.dot(left, right, preferred_element_type=F32)
            square = jnp.maximum(square, 1e-12)
            reach = square * lax.rsqrt(square)
            decay = jnp.exp2(reach * (-CUTOFF * LOG2E))
            taper = jnp.maximum(1.0 - reach, 0.0)
            block = (decay * taper * taper).astype(BF16)
            parts = jnp.concatenate([panel_ref[ha], panel_ref[hb]], axis=0)
            acc = acc + jnp.dot(block, parts, preferred_element_type=F32)
        image = acc * 0.125 + NUGGET * own_ref[g].astype(F32)
        image_ref[g] = image
        high = image.astype(BF16)
        low = (image - high.astype(F32)).astype(BF16)
        both = jnp.concatenate([high, low], axis=1)
        gram_ref[...] += lax.dot_general(
            high, both, (((0,), (0,)), ((), ())), preferred_element_type=F32
        )
        return carry

    lax.fori_loop(0, rows, one_row, 0)


def image_and_gram(cols, left, right, panel, own):
    rows = left.shape[0]
    rank = panel.shape[2]
    vmem = pl.BlockSpec(memory_space=pltpu.VMEM)
    return pl.pallas_call(
        image_kernel,
        name="image",
        out_shape=(
            jax.ShapeDtypeStruct((rows, BS, rank), F32),
            jax.ShapeDtypeStruct((rank, 2 * rank), F32),
        ),
        in_specs=[pl.BlockSpec(memory_space=pltpu.SMEM), vmem, vmem, vmem, vmem],
        out_specs=(vmem, vmem),
        compiler_params=pltpu.CompilerParams(vmem_limit_bytes=48 << 20),
    )(cols, left, right, panel, own)


def place():
    s = lax.axis_index("sector")
    d = lax.axis_index("depth")
    return s // 4, (s // 2) % 2, s % 2, d // 8, d % 8


def all_sum_kernel(total, part_ref, out_ref, got1, got2, got3, mine, whole, s1, r1, s2, r2, s3, r3):
    y, xh, core, xl, z = place()
    q = core * 8 + z
    r = y * 4 + xh * 2 + xl

    def peer_q(k):
        p = lax.rem(q + k, 16)
        return p, (y * 4 + xh * 2 + p // 8, xl * 8 + lax.rem(p, 8))

    def peer_r(k):
        p = lax.rem(r + k, 16)
        return p, ((p // 2) * 2 + core, lax.rem(p, 2) * 8 + z)

    barrier = pltpu.get_barrier_semaphore()

    def greet(k, c):
        pl.semaphore_signal(barrier, inc=1, device_id=peer_q(k)[1], device_id_type=MESH)
        pl.semaphore_signal(barrier, inc=1, device_id=peer_r(k)[1], device_id_type=MESH)
        return c

    lax.fori_loop(1, 16, greet, 0)
    pl.semaphore_wait(barrier, 30)

    def copy1(k):
        p, dev = peer_q(k)
        return pltpu.make_async_remote_copy(
            part_ref.at[p], got1.at[q], s1.at[k], r1.at[k], device_id=dev, device_id_type=MESH
        )

    def copy2(k):
        dev = peer_r(k)[1]
        return pltpu.make_async_remote_copy(
            mine, got2.at[r], s2.at[k], r2.at[k], device_id=dev, device_id_type=MESH
        )

    def copy3(k):
        dev = peer_q(k)[1]
        return pltpu.make_async_remote_copy(
            whole, got3.at[q], s3.at[k], r3.at[k], device_id=dev, device_id_type=MESH
        )

    def start(copy):
        def step(k, c):
            copy(k).start()
            return c

        lax.fori_loop(1, 16, step, 0)

    def arrive(copy):
        def step(k, c):
            copy(k).wait_recv()
            return c

        lax.fori_loop(1, 16, step, 0)

    def leave(copy):
        def step(k, c):
            copy(k).wait_send()
            return c

        lax.fori_loop(1, 16, step, 0)

    start(copy1)
    got1[q] = part_ref[q]
    arrive(copy1)
    mine[...] = jnp.sum(got1[...], axis=0)
    start(copy2)
    got2[r] = mine[...]
    arrive(copy2)
    whole[...] = jnp.sum(got2[...], axis=0) * (1.0 / total)
    start(copy3)
    got3[q] = whole[...]
    arrive(copy3)
    out_ref[...] = got3[...]
    leave(copy1)
    leave(copy2)
    leave(copy3)


def all_sum(part, total):
    vmem = pl.BlockSpec(memory_space=pltpu.VMEM)
    rank = part.shape[1]
    rows = part.shape[0] // 16
    out = pl.pallas_call(
        functools.partial(all_sum_kernel, total),
        name="all_sum",
        out_shape=jax.ShapeDtypeStruct((16, rows, rank), F32),
        in_specs=[vmem],
        out_specs=vmem,
        scratch_shapes=[pltpu.VMEM((16, rows, rank), F32)] * 3
        + [pltpu.VMEM((rows, rank), F32)] * 2
        + [pltpu.SemaphoreType.DMA((16,))] * 6,
        compiler_params=pltpu.CompilerParams(collective_id=1, has_side_effects=True),
    )(part.reshape(16, rows, rank))
    return out.reshape(part.shape)


def nt(a, b):
    return lax.dot_general(
        a, b, (((1,), (1,)), ((), ())), precision=HIGHEST, preferred_element_type=F32
    )


def nn(a, b):
    return jnp.dot(a, b, precision=HIGHEST, preferred_element_type=F32)


def basis_kernel(gram_ref, image_ref, basis_ref, factor_ref, inverse_ref, work_ref):
    n = gram_ref.shape[0]

    @pl.when(pl.program_id(0) == 0)
    def _():
        row = lax.broadcasted_iota(jnp.int32, (n, n), 0)
        col = lax.broadcasted_iota(jnp.int32, (n, n), 1)
        diag = row == col
        weight = jnp.where(row > col, 1.0, jnp.where(diag, 0.5, 0.0)).astype(F32)
        eye = jnp.where(diag, 1.0, 0.0).astype(F32)
        gram = gram_ref[...]
        only = jnp.where(diag, gram, 0.0)
        down = lax.rsqrt(jnp.sum(only, axis=1, keepdims=True))
        across = lax.rsqrt(jnp.sum(only, axis=0, keepdims=True))
        first = gram * down * across - eye
        inverse_ref[...] = (eye - first * weight) * across

        def unsettled(state):
            size, turn = state
            return jnp.logical_and(jnp.logical_not(size < 1e-6), turn < 8)

        def refine(state):
            turn = state[1]
            x = inverse_ref[...]
            gap = nt(nn(x, gram_ref[...]), x) - eye
            inverse_ref[...] = x - nn(gap * weight, x)
            return jnp.sum(gap * gap), turn + 1

        size, _ = lax.while_loop(unsettled, refine, (jnp.sum(first * first), jnp.int32(0)))
        settled = size < 1e-6

        @pl.when(settled)
        def _():
            factor_ref[...] = jnp.where(row <= col, nn(inverse_ref[...], gram_ref[...]), 0.0)

        @pl.when(jnp.logical_not(settled))
        def _():
            work_ref[:, :n] = gram_ref[...]
            work_ref[:, n:] = eye
            wide = lax.broadcasted_iota(jnp.int32, (n, 2 * n), 1)
            tall = lax.broadcasted_iota(jnp.int32, (n, 1), 0)

            def eliminate(k, c):
                m = work_ref[...]
                pivot_row = jnp.sum(jnp.where(tall == k, m, 0.0), axis=0, keepdims=True)
                column = jnp.sum(jnp.where(wide == k, m, 0.0), axis=1, keepdims=True)
                pivot = jnp.sum(jnp.where(tall == k, column, 0.0), axis=0, keepdims=True)
                ratio = jnp.where(tall > k, column / pivot, 0.0)
                work_ref[...] = m - ratio * pivot_row
                return c

            lax.fori_loop(0, n, eliminate, 0)
            upper = work_ref[:, :n]
            scale = lax.rsqrt(jnp.sum(jnp.where(diag, upper, 0.0), axis=1, keepdims=True))
            factor_ref[...] = jnp.where(row <= col, upper * scale, 0.0)
            inverse_ref[...] = work_ref[:, n:] * scale

    x = inverse_ref[...]
    xh = x.astype(BF16)
    xl = (x - xh.astype(F32)).astype(BF16)
    image = image_ref[...]
    high = image.astype(BF16)
    low = (image - high.astype(F32)).astype(BF16)

    def times(a, b):
        return lax.dot_general(a, b, (((1,), (1,)), ((), ())), preferred_element_type=F32)

    basis_ref[...] = times(high, xh) + times(high, xl) + times(low, xh)


def basis_and_factor(gram, image):
    n = gram.shape[0]
    rows = image.shape[0]
    step = 512
    return pl.pallas_call(
        basis_kernel,
        name="basis",
        grid=(rows // step,),
        out_shape=(
            jax.ShapeDtypeStruct((rows, n), F32),
            jax.ShapeDtypeStruct((n, n), F32),
        ),
        in_specs=[
            pl.BlockSpec((n, n), lambda i: (0, 0)),
            pl.BlockSpec((step, n), lambda i: (i, 0)),
        ],
        out_specs=(
            pl.BlockSpec((step, n), lambda i: (i, 0)),
            pl.BlockSpec((n, n), lambda i: (0, 0)),
        ),
        scratch_shapes=[pltpu.VMEM((n, n), F32), pltpu.VMEM((n, 2 * n), F32)],
    )(gram, image)


def on_device(panel, coords, neighbours, ranges):
    block_count = neighbours.shape[0]
    block_size = panel.shape[0] // block_count
    width = panel.shape[1]
    sector_count = lax.axis_size("sector")
    slab_count = lax.axis_size("depth")
    my_sector = lax.axis_index("sector")
    my_slab = lax.axis_index("depth")
    blocked = panel.reshape(block_count, block_size, width)

    low = jnp.stack([my_sector * AZ_SEC, 32, my_slab * DZ + DZ // 2]).astype(jnp.int32)
    inside = (coords - low[:, None]).astype(BF16)
    near = {d: passed_along((blocked, inside), "sector", d) for d in (1, -1)}
    far = {d: passed_along(near[d], "sector", d) for d in (1, -1)}
    ordered = [far[1], near[1], (blocked, inside), near[-1], far[-1]]
    wide_panel = jnp.concatenate([member[0] for member in ordered], axis=0)

    scale = 1.0 / (ranges * CUTOFF) ** 2
    remote = []
    for step, member in enumerate(ordered):
        shift = jnp.array([8.0 * (step - 2) - 4.0, 0.0, 0.0], F32)
        place3 = member[1].astype(F32) + shift[:, None]
        norm = jnp.sum(scale[:, None] * place3 * place3, axis=0)
        n1, n2, n3 = pieces(norm)
        one = jnp.ones_like(norm)
        zero = jnp.zeros_like(norm)
        rows = jnp.concatenate(
            [place3, place3, place3, jnp.stack([one, one, one, n1, n2, n3, zero])], axis=0
        )
        remote.append(rows.reshape(16, block_count, block_size))
        if step == 2:
            a1, a2, a3 = pieces(-2.0 * scale[:, None] * place3)
            home = jnp.concatenate(
                [a1, a2, a3, jnp.stack([n1, n2, n3, one, one, one, zero])], axis=0
            )
            home = home.astype(BF16).reshape(16, block_count, block_size)
    right = jnp.transpose(jnp.concatenate(remote, axis=1).astype(BF16), (1, 0, 2))
    left = jnp.transpose(home, (1, 2, 0))

    column_sector = neighbours // (slab_count * block_count)
    step_away = (column_sector - my_sector + 2) % sector_count
    local_column = step_away * block_count + neighbours % block_count

    image, gram2 = image_and_gram(local_column, left, right, wide_panel, blocked)
    cross = gram2[:, width:]
    part = gram2[:, :width] + cross + cross.T
    image = image.reshape(block_count * block_size, width)
    total_cells = float(image.shape[0] * sector_count * slab_count)
    gram = all_sum(part, total_cells)
    basis, factor = basis_and_factor(gram, image)
    return (basis, factor)


def solution(mesh):
    in_specs = (
        P(("sector", "depth"), None),
        P(None, ("sector", "depth")),
        P(("sector", "depth"), None),
        P(),
    )
    out_specs = (P(("sector", "depth"), None), P())
    return jax.shard_map(
        on_device, mesh=mesh, in_specs=in_specs, out_specs=out_specs, check_vma=False
    )
```

time: 626 us -> 179 us (0.29)
  waiting for transfers between devices: 278 us -> 18.7 us
  matrix products: 128 us -> 0 us
  other arithmetic: 119 us -> 3.76 us
  Pallas kernels: 0 us -> 102 us
  local copies, waits for them, and re-layouts: 65.2 us -> 33.7 us
  between operations: 14.2 us -> 0.95 us
    psum x1 -> x0, waiting for transfers between devices: 242 us -> none  [on_device(): lower = jnp.linalg.cholesky(lax.psum(local_gram, ('sector', 'depth')))]
    dot_general x10 -> x0, matrix products: 127 us -> none  [the longest x8 120 us: one_group(): jnp.einsum('gnab,gnbc->gac', kernel, wide_panel[rows_list], preferred_ele...]
    pallas_call x0 -> x3, Pallas kernels: none -> 102 us  [the longest x1 46.2 us: image_and_gram(): pl.pallas_call(image_kernel, name='image', out_shape=(jax.ShapeDtypeStruc...]
    convert_element_type x8 -> x0, other arithmetic: 94.5 us -> none  [cov_blocks(): (home[:, None, :, :, None] - remote[:, :, :, None, :]).astype(jnp.float32)]
    gather x24 -> x0, local copies, waits for them, and re-layouts: 50.9 us -> none  [the longest x8 44.8 us: one_group(): wide_panel[rows_list]]
    another operation x4 -> x7, other arithmetic: 22.2 us -> 1.22 us  [the longest x3 12.4 us: on_device(): lower = jnp.linalg.cholesky(lax.psum(local_gram, ('sector', 'depth')))]
    ppermute x8, waiting for transfers between devices: 35.2 us -> 18.7 us  [passed_along(): return lax.ppermute(block, axis, route)]
    concatenate x1 -> x13, local copies, waits for them, and re-layouts: 0.01 us -> 15.8 us  [the longest x7 13.4 us: on_device(): jnp.concatenate([a1, a2, a3, jnp.stack([n1, n2, n3, one, one, one, zero])...]
  transfers between devices with their start and end apart: 9 -> 8, of which waited for: 5 -> 2; matrix products, arithmetic and copies ran while one was open for 1% -> 17% of each run, Pallas kernels for 0% -> 0%
where the time goes in v1:
time: 179 us; the launch traced here: 178 us
  Pallas kernels  102 us (57%)
  local copies, waits for them, and re-layouts  33.7 us (19%)
  starting transfers between devices  18.7 us (10%)
  waiting for transfers between devices  18.7 us (10%)
  other arithmetic  3.76 us (2%)
    pallas_call x1, Pallas kernels, image_and_gram(): pl.pallas_call(image_kernel, name='image', out_shape=(jax.ShapeDtypeStruc...  46.2 us
    pallas_call x1, Pallas kernels, basis_and_factor(): pl.pallas_call(basis_kernel, name='basis', grid=(rows // step,), out_shap...  29.4 us
    pallas_call x1, Pallas kernels, all_sum(): pl.pallas_call(functools.partial(all_sum_kernel, total), name='all_sum',...  26.3 us
    ppermute x8, waiting for transfers between devices, passed_along(): return lax.ppermute(block, axis, route)  18.7 us
    ppermute x8, starting transfers between devices, passed_along(): return lax.ppermute(block, axis, route)  18.7 us
    concatenate x7, local copies, waits for them, and re-layouts, on_device(): jnp.concatenate([a1, a2, a3, jnp.stack([n1, n2, n3, one, one, one, zero])...  13.4 us
    unnamed x14, local copies, waits for them, and re-layouts  8.07 us
    another operation x6, local copies, waits for them, and re-layouts  7.56 us
  transfers between devices with their start and end apart: 8, of which 2 were waited for; matrix products, arithmetic and copies ran while one was open for 17% of the time, Pallas kernels for 0%

profile of v1, /device:TPU:1, one launch (start us, length us, event | category | flops | bytes accessed | tf_op | source)
XLA Modules:
  0.0 177.7 jit_solution(8699923053236056716)
XLA Ops:
  0.6 0.1 pad_add_fusion
  0.7 1.0 fusion.13
  1.7 4.2 %collective-permute-start = (bf16[3,4096]{1,0:T(4,128)(2,1)S(1)}, bf16[3,4096]{1,0:T(4,128)(2,1)S(1)}, u32[]{:S(2)}, u32[]{:S(2)}) collective-permute-start(bf16[3,4096]{1,0:T(4,128)(2,1)S(1)} %get-tuple-element.12), channel_id=1, source_target_pairs={{240,0},{0,16},{16,32},{32,48},{48,64},{64,80},{80,96},{96,112},{1... | collective-permute-start | bytes 73736 | tf_op jit(solution)/shard_map/ppermute | solution.py:25
  5.9 0.0 collective-permute-start.2
  5.9 3.2 %collective-permute-start.4 = (bf16[32,128,128]{2,1,0:T(8,128)(2,1)}, bf16[32,128,128]{2,1,0:T(8,128)(2,1)}, u32[]{:S(2)}, u32[]{:S(2)}) collective-permute-start(bf16[32,128,128]{2,1,0:T(8,128)(2,1)} %bitcast.29), channel_id=1, source_target_pairs={{240,0},{0,16},{16,32},{32,48},{48,64},{64,80},{80,96},{96,112},{1... | collective-permute-start | bytes 3145736 | tf_op jit(solution)/shard_map/ppermute | solution.py:25
  9.1 1.2 collective-permute-start.6
  10.3 0.7 fusion.28.cols
  11.1 0.0 collective-permute-done
  11.1 2.1 %collective-permute-start.1 = (bf16[3,4096]{1,0:T(4,128)(2,1)S(1)}, bf16[3,4096]{1,0:T(4,128)(2,1)S(1)}, u32[]{:S(2)}, u32[]{:S(2)}) collective-permute-start(bf16[3,4096]{1,0:T(4,128)(2,1)S(1)} %collective-permute-done), channel_id=1, source_target_pairs={{240,0},{0,16},{16,32},{32,48},{48,64},{64,80},{80,96},{96,112},{1... | collective-permute-start | bytes 73736 | tf_op jit(solution)/shard_map/ppermute | solution.py:25
  13.2 0.0 collective-permute-done.2
  13.2 3.4 %collective-permute-start.3 = (bf16[3,4096]{1,0:T(4,128)(2,1)S(1)}, bf16[3,4096]{1,0:T(4,128)(2,1)S(1)}, u32[]{:S(2)}, u32[]{:S(2)}) collective-permute-start(bf16[3,4096]{1,0:T(4,128)(2,1)S(1)} %collective-permute-done.2), channel_id=1, source_target_pairs={{16,0},{32,16},{48,32},{64,48},{80,64},{96,80},{112,96},{128,112},... | collective-permute-start | bytes 73736 | tf_op jit(solution)/shard_map/ppermute | solution.py:25
  16.6 0.7 broadcast_multiply_fusion
  17.3 9.6 %collective-permute-done.1 = bf16[3,4096]{1,0:T(4,128)(2,1)S(1)} collective-permute-done((bf16[3,4096]{1,0:T(4,128)(2,1)S(1)}, bf16[3,4096]{1,0:T(4,128)(2,1)S(1)}, u32[]{:S(2)}, u32[]{:S(2)}) %collective-permute-start.1) | collective-permute-done | bytes 24608 | tf_op jit(solution)/shard_map/ppermute | solution.py:25
  26.9 9.1 %collective-permute-done.3 = bf16[3,4096]{1,0:T(4,128)(2,1)S(1)} collective-permute-done((bf16[3,4096]{1,0:T(4,128)(2,1)S(1)}, bf16[3,4096]{1,0:T(4,128)(2,1)S(1)}, u32[]{:S(2)}, u32[]{:S(2)}) %collective-permute-start.3) | collective-permute-done | bytes 24608 | tf_op jit(solution)/shard_map/ppermute | solution.py:25
  36.0 1.1 fusion.5
  37.2 0.1 collective-permute-start.5
  37.4 0.5 concatenate.67
  38.0 0.0 collective-permute-done.6
  38.0 4.4 %collective-permute-start.7 = (bf16[32,128,128]{2,1,0:T(8,128)(2,1)}, bf16[32,128,128]{2,1,0:T(8,128)(2,1)}, u32[]{:S(2)}, u32[]{:S(2)}) collective-permute-start(bf16[32,128,128]{2,1,0:T(8,128)(2,1)} %collective-permute-done.6), channel_id=1, source_target_pairs={{16,0},{32,16},{48,32},{64,48},{80,64},{96,80},{112,96},{128,112},... | collective-permute-start | bytes 3145736 | tf_op jit(solution)/shard_map/ppermute | solution.py:25
  42.4 0.5 copy.48
  43.0 1.4 copy.49
  44.4 1.4 copy.50
  45.8 0.5 concatenate.71
  46.3 1.4 copy.45
  47.7 1.4 copy.46
  49.1 1.4 copy.47
  50.5 0.5 concatenate.69
  51.0 0.5 concatenate.73
  51.5 0.5 concatenate.75
  52.0 1.3 concatenate.62.clone
  53.2 1.2 concatenate.63.clone
  54.4 1.2 concatenate.64.clone
  55.6 9.6 %concatenate.65 = bf16[16,32,128]{0,2,1:T(8,128)(2,1)S(1)} concatenate(bf16[3,32,128]{0,2,1:T(8,128)(2,1)} %bitcast.35, bf16[3,32,128]{0,2,1:T(8,128)(2,1)} %bitcast.36, bf16[3,32,128]{0,2,1:T(8,128)(2,1)} %bitcast.37, bf16[1,32,128]{0,2,1:T(8,128)(2,1)S(1)} %copy.48, bf16[1,32,128]{0,2,1:T(8,128)(2,1)} %copy.49, bf16[1,32,128]{0,2,1:T(8,128)(2,1)} %copy.50, ...), dimensions={0} | concatenate | bytes 262144 | tf_op jit(solution)/shard_map/concatenate | solution.py:325
  65.3 0.0 copy-start
  65.4 0.0 collective-permute-done.5
  65.4 1.4 constant_dynamic-update-slice_fusion.9
  66.8 1.4 constant_dynamic-update-slice_fusion.8
  68.2 0.2 constant_dynamic-update-slice_fusion.7
  68.4 1.4 constant_dynamic-update-slice_fusion.6
  69.9 1.4 constant_dynamic-update-slice_fusion.5.panel_ref
  71.3 2.3 %copy-done.2 = bf16[160,128,128]{2,1,0:T(8,128)(2,1)} copy-done((bf16[160,128,128]{2,1,0:T(8,128)(2,1)}, bf16[160,128,128]{2,1,0:T(8,128)(2,1)S(1)}, u32[]{:S(2)}) %copy-start.2) | copy-done | bytes 5242904
  73.6 46.2 %image.1 = (f32[32,128,128]{2,1,0:T(8,128)S(1)}, f32[128,256]{1,0:T(8,128)S(1)}) custom-call(s32[32,32]{1,0:T(8,128)S(1)} %fusion.28.cols, bf16[32,128,16]{2,1,0:T(8,128)(2,1)S(1)} %bitcast.28, bf16[160,16,128]{2,1,0:T(8,128)(2,1)S(1)} %bitcast.34, bf16[160,128,128]{2,1,0:T(8,128)(2,1)} %copy-done.2, bf16[32,128,128]{2,1,0:T(8,128)(2,1)S(1)} %bitcast.32), custom_call_target="tpu_custom_call" | custom-call | tf_op jit(solution)/shard_map/image/pallas_call | solution.py:73
  119.7 1.3 copy-done.1
  121.1 0.1 copy.54
  121.2 0.1 copy.55
  121.3 0.7 copy.56
  122.0 26.3 %all_sum.1 = f32[16,8,128]{2,1,0:T(8,128)} custom-call(f32[16,8,128]{2,1,0:T(8,128)} %bitcast.39), custom_call_target="tpu_custom_call" | custom-call | tf_op jit(solution)/shard_map/all_sum/pallas_call | solution.py:175
  148.3 29.4 %basis.1 = (f32[4096,128]{1,0:T(8,128)}, f32[128,128]{1,0:T(8,128)}) custom-call(f32[128,128]{1,0:T(8,128)} %bitcast.38, f32[4096,128]{1,0:T(8,128)} %bitcast.33), custom_call_target="tpu_custom_call" | custom-call | tf_op jit(solution)/shard_map/basis/pallas_call | solution.py:273
  (20 shorter events, 0.4 us)
Async XLA Ops:
  1.7 9.4 %collective-permute-start = (bf16[3,4096]{1,0:T(4,128)(2,1)S(1)}, bf16[3,4096]{1,0:T(4,128)(2,1)S(1)}, u32[]{:S(2)}, u32[]{:S(2)}) collective-permute-start(bf16[3,4096]{1,0:T(4,128)(2,1)S(1)} %get-tuple-element.12), channel_id=1, source_target_pairs={{240,0},{0,16},{16,32},{32,48},{48,64},{64,80},{80,96},{96,112},{1... | collective-permute-start | bytes 73736 | tf_op jit(solution)/shard_map/ppermute | solution.py:25
  5.9 7.3 %collective-permute-start.2 = (bf16[3,4096]{1,0:T(4,128)(2,1)S(1)}, bf16[3,4096]{1,0:T(4,128)(2,1)S(1)}, u32[]{:S(2)}, u32[]{:S(2)}) collective-permute-start(bf16[3,4096]{1,0:T(4,128)(2,1)S(1)} %get-tuple-element.12), channel_id=1, source_target_pairs={{16,0},{32,16},{48,32},{64,48},{80,64},{96,80},{112,96},{128,112},... | collective-permute-start | bytes 73736 | tf_op jit(solution)/shard_map/ppermute | solution.py:25
  5.9 31.3 %collective-permute-start.4 = (bf16[32,128,128]{2,1,0:T(8,128)(2,1)}, bf16[32,128,128]{2,1,0:T(8,128)(2,1)}, u32[]{:S(2)}, u32[]{:S(2)}) collective-permute-start(bf16[32,128,128]{2,1,0:T(8,128)(2,1)} %bitcast.29), channel_id=1, source_target_pairs={{240,0},{0,16},{16,32},{32,48},{48,64},{64,80},{80,96},{96,112},{1... | collective-permute-start | bytes 3145736 | tf_op jit(solution)/shard_map/ppermute | solution.py:25
  9.1 28.9 %collective-permute-start.6 = (bf16[32,128,128]{2,1,0:T(8,128)(2,1)}, bf16[32,128,128]{2,1,0:T(8,128)(2,1)}, u32[]{:S(2)}, u32[]{:S(2)}) collective-permute-start(bf16[32,128,128]{2,1,0:T(8,128)(2,1)} %bitcast.30), channel_id=1, source_target_pairs={{16,0},{32,16},{48,32},{64,48},{80,64},{96,80},{112,96},{128,112},... | collective-permute-start | bytes 3145736 | tf_op jit(solution)/shard_map/ppermute | solution.py:25
  11.1 15.8 %collective-permute-start.1 = (bf16[3,4096]{1,0:T(4,128)(2,1)S(1)}, bf16[3,4096]{1,0:T(4,128)(2,1)S(1)}, u32[]{:S(2)}, u32[]{:S(2)}) collective-permute-start(bf16[3,4096]{1,0:T(4,128)(2,1)S(1)} %collective-permute-done), channel_id=1, source_target_pairs={{240,0},{0,16},{16,32},{32,48},{48,64},{64,80},{80,96},{96,112},{1... | collective-permute-start | bytes 73736 | tf_op jit(solution)/shard_map/ppermute | solution.py:25
  13.2 22.8 %collective-permute-start.3 = (bf16[3,4096]{1,0:T(4,128)(2,1)S(1)}, bf16[3,4096]{1,0:T(4,128)(2,1)S(1)}, u32[]{:S(2)}, u32[]{:S(2)}) collective-permute-start(bf16[3,4096]{1,0:T(4,128)(2,1)S(1)} %collective-permute-done.2), channel_id=1, source_target_pairs={{16,0},{32,16},{48,32},{64,48},{80,64},{96,80},{112,96},{128,112},... | collective-permute-start | bytes 73736 | tf_op jit(solution)/shard_map/ppermute | solution.py:25
  37.2 28.2 %collective-permute-start.5 = (bf16[32,128,128]{2,1,0:T(8,128)(2,1)}, bf16[32,128,128]{2,1,0:T(8,128)(2,1)}, u32[]{:S(2)}, u32[]{:S(2)}) collective-permute-start(bf16[32,128,128]{2,1,0:T(8,128)(2,1)} %collective-permute-done.4), channel_id=1, source_target_pairs={{240,0},{0,16},{16,32},{32,48},{48,64},{64,80},{80,96},{96,112},{1... | collective-permute-start | bytes 3145736 | tf_op jit(solution)/shard_map/ppermute | solution.py:25
  38.0 31.8 %collective-permute-start.7 = (bf16[32,128,128]{2,1,0:T(8,128)(2,1)}, bf16[32,128,128]{2,1,0:T(8,128)(2,1)}, u32[]{:S(2)}, u32[]{:S(2)}) collective-permute-start(bf16[32,128,128]{2,1,0:T(8,128)(2,1)} %collective-permute-done.6), channel_id=1, source_target_pairs={{16,0},{32,16},{48,32},{64,48},{80,64},{96,80},{112,96},{128,112},... | collective-permute-start | bytes 3145736 | tf_op jit(solution)/shard_map/ppermute | solution.py:25
  65.3 2.9 %copy-start = (bf16[4096,128]{1,0:T(8,128)(2,1)S(1)}, bf16[4096,128]{1,0:T(8,128)(2,1)}, u32[]{:S(2)}) copy-start(bf16[4096,128]{1,0:T(8,128)(2,1)} %param.9) | copy-start | bytes 3145732
  71.3 2.3 %copy-start.2 = (bf16[160,128,128]{2,1,0:T(8,128)(2,1)}, bf16[160,128,128]{2,1,0:T(8,128)(2,1)S(1)}, u32[]{:S(2)}) copy-start(bf16[160,128,128]{2,1,0:T(8,128)(2,1)S(1)} %constant_dynamic-update-slice_fusion.5.panel_ref) | copy-start | bytes 15728644
  119.7 1.3 copy-start.1

commit v2 on v1

v2 whole, which is shorter than its diff:
```python
import functools
import math

import jax
import jax.numpy as jnp
from jax import lax
from jax.experimental import pallas as pl
from jax.experimental.pallas import tpu as pltpu
from jax.sharding import PartitionSpec as P

AZ_SEC = 8
DZ = 8
CUTOFF = 3.0
NUGGET = 0.5
BS = 128
LOG2E = 1.4426950408889634
MESH = pl.DeviceIdType.MESH
F32 = jnp.float32
BF16 = jnp.bfloat16
HIGHEST = lax.Precision.HIGHEST


STEPS = 5


def place():
    s = lax.axis_index("sector")
    d = lax.axis_index("depth")
    return s // 4, (s // 2) % 2, s % 2, d // 8, d % 8


def short(value):
    return value.astype(BF16).astype(F32)


def pieces(value):
    one = short(value)
    two = short(value - one)
    return one, two, value - one - two


def image_kernel(
    total, cols, scale, mine_ref, own_ref, image_ref, gram_ref,
    block_ref, wide_ref, place_ref, right_ref, left_ref, local_ref,
    part_ref, got1, got2, got3, mine, whole,
    place_s, place_r, cross_s, cross_r, along_s, along_r, twin_s, twin_r, own_s, own_r,
    s1, r1, s2, r2, s3, r3,
):
    rows, rank = own_ref.shape[0], own_ref.shape[2]
    slots = cols.shape[1]
    chunks = cross_s.shape[0]
    size = rows // chunks
    y, xh, core, xl, z = place()
    s = lax.axis_index("sector")
    d = lax.axis_index("depth")
    q = core * 8 + z
    r = y * 4 + xh * 2 + xl

    def sector(k):
        return lax.rem(s + k + 16, 16), d

    def peer_q(k):
        p = lax.rem(q + k, 16)
        return p, (y * 4 + xh * 2 + p // 8, xl * 8 + lax.rem(p, 8))

    def peer_r(k):
        p = lax.rem(r + k, 16)
        return p, ((p // 2) * 2 + core, lax.rem(p, 2) * 8 + z)

    barrier = pltpu.get_barrier_semaphore()
    for k in (-2, -1, 1, 2, -4, 4):
        pl.semaphore_signal(barrier, inc=1, device_id=sector(k), device_id_type=MESH)

    def greet(k, c):
        pl.semaphore_signal(barrier, inc=1, device_id=peer_q(k)[1], device_id_type=MESH)
        pl.semaphore_signal(barrier, inc=1, device_id=peer_r(k)[1], device_id_type=MESH)
        return c

    lax.fori_loop(1, 16, greet, 0)
    pl.semaphore_wait(barrier, 36)

    opposite = sector(2 - 4 * xh)
    onward = sector(4 - 8 * xh)
    across_at = (4 - 4 * xh) * rows
    along_at = 4 * xh * rows
    twin = sector(1 - 2 * core)
    twin_from = (4 - 4 * core) * rows
    twin_to = (3 - 2 * core) * rows
    own_to = (1 + 2 * core) * rows

    def remote(src, dst, send, recv, dev):
        return pltpu.make_async_remote_copy(
            src, dst, send, recv, device_id=dev, device_id_type=MESH
        )

    def place_copy(i):
        k = (-2, -1, 1, 2)[i]
        return remote(mine_ref, place_ref.at[2 - k], place_s.at[i], place_r.at[i], sector(k))

    def cross_copy(c):
        return remote(
            own_ref.at[pl.ds(c * size, size)],
            wide_ref.at[pl.ds(4 * xh * rows + c * size, size)],
            cross_s.at[c], cross_r.at[c], opposite,
        )

    def along_copy(c):
        return remote(
            wide_ref.at[pl.ds(across_at + c * size, size)],
            wide_ref.at[pl.ds(along_at + c * size, size)],
            along_s.at[c], along_r.at[c], onward,
        )

    def twin_copy(c):
        return remote(
            wide_ref.at[pl.ds(twin_from + c * size, size)],
            wide_ref.at[pl.ds(twin_to + c * size, size)],
            twin_s.at[c], twin_r.at[c], twin,
        )

    def own_copy():
        return remote(own_ref, wide_ref.at[pl.ds(own_to, rows)], own_s, own_r, twin)

    def every(count, do):
        def step(k, c):
            do(k)
            return c

        lax.fori_loop(0, count, step, 0)

    for i in range(4):
        place_copy(i).start()
    every(chunks, lambda c: cross_copy(c).start())
    own_copy().start()
    wide_ref[pl.ds(2 * rows, rows)] = own_ref[...]
    local_ref[...] = jnp.zeros_like(local_ref)

    line = lax.broadcasted_iota(jnp.int32, (1, 8, BS), 1)
    w = jnp.where(line == 0, scale[0], jnp.where(line == 1, scale[1], scale[2]))
    w = jnp.where(line < 3, w, 0.0)

    def spread(ref_value, step):
        even = ref_value.astype(F32).reshape(rows // 2, 8, BS)
        odd = jnp.concatenate([even[:, 4:], even[:, :4]], axis=1)
        both = jnp.stack([even, odd], axis=1).reshape(rows, 8, BS)
        both = both + jnp.where(line == 0, 8.0 * (step - 2) - 4.0, 0.0)
        norm = jnp.sum(both * both * w, axis=1, keepdims=True)
        return both, norm

    def put_right(both, norm, step):
        n1, n2, n3 = pieces(norm)
        tail = jnp.where(line == 4, n1, jnp.where(line == 5, n2, jnp.where(line == 6, n3, 0.0)))
        base = jnp.where(line < 4, both, tail)
        twice = jnp.concatenate([base, base], axis=1).astype(BF16)
        right_ref[pl.ds(step * rows, rows)] = twice

    both, norm = spread(mine_ref[...], 2)
    put_right(both, norm, 2)
    full = jnp.where(line < 3, -2.0 * w * both, jnp.where(line == 3, norm, 0.0))
    a1, a2, a3 = pieces(full)
    a1 = a1 + jnp.where(jnp.logical_and(line > 3, line < 7), 1.0, 0.0)
    left_ref[...] = jnp.concatenate([a1, a2, a3, jnp.zeros_like(a1)], axis=1)
    for i in range(4):
        place_copy(i).wait_recv()
    for step in (0, 1, 3, 4):
        both, norm = spread(place_ref[step], step)
        put_right(both, norm, step)

    def build(g):
        left = jnp.transpose(left_ref[g]).astype(BF16)
        for n in range(0, slots, 2):
            right = jnp.concatenate([right_ref[cols[g, n]], right_ref[cols[g, n + 1]]], axis=1)
            right = jnp.concatenate([right, right], axis=0)
            square = jnp.dot(left, right, preferred_element_type=F32)
            square = jnp.maximum(square, 1e-10)
            rest = CUTOFF * LOG2E - square * lax.rsqrt(square)
            taper = jnp.maximum(rest, 0.0)
            block = jnp.exp2(rest) * taper * taper
            block_ref[g, :, n * BS : (n + 2) * BS] = block.astype(BF16)

    lag = 2

    def turn(c, carry):
        every(size, lambda i: build(c * size + i))
        cross_copy(c).wait_recv()
        along_copy(c).start()

        @pl.when(c >= lag)
        def _():
            along_copy(c - lag).wait_recv()
            twin_copy(c - lag).start()

        return carry

    lax.fori_loop(0, chunks, turn, 0)

    def tail(i):
        along_copy(chunks - lag + i).wait_recv()
        twin_copy(chunks - lag + i).start()

    every(lag, tail)
    own_copy().wait_recv()
    every(chunks, lambda c: twin_copy(c).wait_recv())

    factor = math.exp(-CUTOFF) / (8.0 * (CUTOFF * LOG2E) ** 2)

    def multiply(g):
        acc = jnp.zeros((BS, rank), F32)
        for n in range(0, slots, 2):
            parts = jnp.concatenate([wide_ref[cols[g, n]], wide_ref[cols[g, n + 1]]], axis=0)
            acc = acc + jnp.dot(
                block_ref[g, :, n * BS : (n + 2) * BS], parts, preferred_element_type=F32
            )
        image = acc * factor + NUGGET * own_ref[g].astype(F32)
        image_ref[g] = image
        high = image.astype(BF16)
        low = (image - high.astype(F32)).astype(BF16)
        pair = jnp.concatenate([high, low], axis=1)
        local_ref[...] += lax.dot_general(
            high, pair, (((0,), (0,)), ((), ())), preferred_element_type=F32
        )

    every(rows, multiply)
    cross = local_ref[:, rank:]
    part = local_ref[:, :rank] + cross + jnp.transpose(cross)
    part_ref[...] = part.reshape(part_ref.shape)

    def copy1(k):
        p, dev = peer_q(k)
        return remote(part_ref.at[p], got1.at[q], s1.at[k], r1.at[k], dev)

    def copy2(k):
        return remote(mine, got2.at[r], s2.at[k], r2.at[k], peer_r(k)[1])

    def copy3(k):
        return remote(whole, got3.at[q], s3.at[k], r3.at[k], peer_q(k)[1])

    def others(do):
        def step(k, c):
            do(k)
            return c

        lax.fori_loop(1, 16, step, 0)

    others(lambda k: copy1(k).start())
    got1[q] = part_ref[q]
    others(lambda k: copy1(k).wait_recv())
    mine[...] = jnp.sum(got1[...], axis=0)
    others(lambda k: copy2(k).start())
    got2[r] = mine[...]
    others(lambda k: copy2(k).wait_recv())
    whole[...] = jnp.sum(got2[...], axis=0) * (1.0 / total)
    others(lambda k: copy3(k).start())
    got3[q] = whole[...]
    others(lambda k: copy3(k).wait_recv())
    gram_ref[...] = got3[...]

    for i in range(4):
        place_copy(i).wait_send()
    own_copy().wait_send()
    every(chunks, lambda c: cross_copy(c).wait_send())
    every(chunks, lambda c: along_copy(c).wait_send())
    every(chunks, lambda c: twin_copy(c).wait_send())
    others(lambda k: copy1(k).wait_send())
    others(lambda k: copy2(k).wait_send())
    others(lambda k: copy3(k).wait_send())


def image_and_gram(cols, scale, mine, own, total):
    rows, size, rank = own.shape
    slots = cols.shape[1]
    chunks = 16
    vmem = pl.BlockSpec(memory_space=pltpu.VMEM)
    smem = pl.BlockSpec(memory_space=pltpu.SMEM)
    dma = pltpu.SemaphoreType.DMA
    piece = rank // 16
    image, gram = pl.pallas_call(
        functools.partial(image_kernel, total),
        name="image",
        out_shape=(
            jax.ShapeDtypeStruct((rows, size, rank), F32),
            jax.ShapeDtypeStruct((16, piece, rank), F32),
        ),
        in_specs=[smem, smem, vmem, vmem],
        out_specs=(vmem, vmem),
        scratch_shapes=[
            pltpu.VMEM((rows, size, slots * size), BF16),
            pltpu.VMEM((STEPS * rows, size, rank), BF16),
            pltpu.VMEM((STEPS, rows * 4, size), BF16),
            pltpu.VMEM((STEPS * rows, 16, size), BF16),
            pltpu.VMEM((rows, 32, size), F32),
            pltpu.VMEM((rank, 2 * rank), F32),
        ]
        + [pltpu.VMEM((16, piece, rank), F32)] * 4
        + [pltpu.VMEM((piece, rank), F32)] * 2
        + [dma((4,))] * 2
        + [dma((chunks,))] * 6
        + [dma(())] * 2
        + [dma((16,))] * 6,
        compiler_params=pltpu.CompilerParams(
            collective_id=1, has_side_effects=True, vmem_limit_bytes=58 << 20
        ),
    )(cols, scale, mine, own)
    return image, gram.reshape(rank, rank)


def nt(a, b):
    return lax.dot_general(
        a, b, (((1,), (1,)), ((), ())), precision=HIGHEST, preferred_element_type=F32
    )


def nn(a, b):
    return jnp.dot(a, b, precision=HIGHEST, preferred_element_type=F32)


def basis_kernel(gram_ref, image_ref, basis_ref, factor_ref, inverse_ref, work_ref):
    n = gram_ref.shape[0]

    @pl.when(pl.program_id(0) == 0)
    def _():
        row = lax.broadcasted_iota(jnp.int32, (n, n), 0)
        col = lax.broadcasted_iota(jnp.int32, (n, n), 1)
        diag = row == col
        weight = jnp.where(row > col, 1.0, jnp.where(diag, 0.5, 0.0)).astype(F32)
        eye = jnp.where(diag, 1.0, 0.0).astype(F32)
        gram = gram_ref[...]
        only = jnp.where(diag, gram, 0.0)
        down = lax.rsqrt(jnp.sum(only, axis=1, keepdims=True))
        across = lax.rsqrt(jnp.sum(only, axis=0, keepdims=True))
        first = gram * down * across - eye
        inverse_ref[...] = (eye - first * weight) * across

        def unsettled(state):
            size, turn = state
            return jnp.logical_and(jnp.logical_not(size < 1e-6), turn < 8)

        def refine(state):
            turn = state[1]
            x = inverse_ref[...]
            gap = nt(nn(x, gram_ref[...]), x) - eye
            inverse_ref[...] = x - nn(gap * weight, x)
            return jnp.sum(gap * gap), turn + 1

        size, _ = lax.while_loop(unsettled, refine, (jnp.sum(first * first), jnp.int32(0)))
        settled = size < 1e-6

        @pl.when(settled)
        def _():
            factor_ref[...] = jnp.where(row <= col, nn(inverse_ref[...], gram_ref[...]), 0.0)

        @pl.when(jnp.logical_not(settled))
        def _():
            work_ref[:, :n] = gram_ref[...]
            work_ref[:, n:] = eye
            wide = lax.broadcasted_iota(jnp.int32, (n, 2 * n), 1)
            tall = lax.broadcasted_iota(jnp.int32, (n, 1), 0)

            def eliminate(k, c):
                m = work_ref[...]
                pivot_row = jnp.sum(jnp.where(tall == k, m, 0.0), axis=0, keepdims=True)
                column = jnp.sum(jnp.where(wide == k, m, 0.0), axis=1, keepdims=True)
                pivot = jnp.sum(jnp.where(tall == k, column, 0.0), axis=0, keepdims=True)
                ratio = jnp.where(tall > k, column / pivot, 0.0)
                work_ref[...] = m - ratio * pivot_row
                return c

            lax.fori_loop(0, n, eliminate, 0)
            upper = work_ref[:, :n]
            scale = lax.rsqrt(jnp.sum(jnp.where(diag, upper, 0.0), axis=1, keepdims=True))
            factor_ref[...] = jnp.where(row <= col, upper * scale, 0.0)
            inverse_ref[...] = work_ref[:, n:] * scale

    x = inverse_ref[...]
    xh = x.astype(BF16)
    xl = (x - xh.astype(F32)).astype(BF16)
    image = image_ref[...]
    high = image.astype(BF16)
    low = (image - high.astype(F32)).astype(BF16)

    def times(a, b):
        return lax.dot_general(a, b, (((1,), (1,)), ((), ())), preferred_element_type=F32)

    basis_ref[...] = times(high, xh) + times(high, xl) + times(low, xh)


def basis_and_factor(gram, image):
    n = gram.shape[0]
    rows = image.shape[0]
    step = 512
    return pl.pallas_call(
        basis_kernel,
        name="basis",
        grid=(rows // step,),
        out_shape=(
            jax.ShapeDtypeStruct((rows, n), F32),
            jax.ShapeDtypeStruct((n, n), F32),
        ),
        in_specs=[
            pl.BlockSpec((n, n), lambda i: (0, 0)),
            pl.BlockSpec((step, n), lambda i: (i, 0)),
        ],
        out_specs=(
            pl.BlockSpec((step, n), lambda i: (i, 0)),
            pl.BlockSpec((n, n), lambda i: (0, 0)),
        ),
        scratch_shapes=[pltpu.VMEM((n, n), F32), pltpu.VMEM((n, 2 * n), F32)],
    )(gram, image)


def on_device(panel, coords, neighbours, ranges):
    block_count = neighbours.shape[0]
    block_size = panel.shape[0] // block_count
    width = panel.shape[1]
    sector_count = lax.axis_size("sector")
    slab_count = lax.axis_size("depth")
    my_sector = lax.axis_index("sector")
    my_slab = lax.axis_index("depth")
    blocked = panel.reshape(block_count, block_size, width)

    low = jnp.stack([my_sector * AZ_SEC, 32, my_slab * DZ + DZ // 2]).astype(jnp.int32)
    inside = (coords - low[:, None]).reshape(3, block_count, block_size)
    inside = jnp.concatenate([inside, jnp.ones_like(inside[:1])], axis=0)
    mine = jnp.transpose(inside, (1, 0, 2)).reshape(4 * block_count, block_size).astype(BF16)
    scale = (LOG2E / ranges) ** 2

    column_sector = neighbours // (slab_count * block_count)
    step_away = (column_sector - my_sector + 2) % sector_count
    local_column = step_away * block_count + neighbours % block_count

    total_cells = float(panel.shape[0] * sector_count * slab_count)
    image, gram = image_and_gram(local_column, scale, mine, blocked, total_cells)
    image = image.reshape(block_count * block_size, width)
    basis, factor = basis_and_factor(gram, image)
    return (basis, factor)


def solution(mesh):
    in_specs = (
        P(("sector", "depth"), None),
        P(None, ("sector", "depth")),
        P(("sector", "depth"), None),
        P(),
    )
    out_specs = (P(("sector", "depth"), None), P())
    return jax.shard_map(
        on_device, mesh=mesh, in_specs=in_specs, out_specs=out_specs, check_vma=False
    )
```

time: 179 us -> 125 us (0.70)
  local copies, waits for them, and re-layouts: 33.7 us -> 0.63 us
  starting transfers between devices: 18.7 us -> 0 us
  waiting for transfers between devices: 18.7 us -> 0 us
  Pallas kernels: 102 us -> 120 us
    ppermute x8 -> x0, waiting for transfers between devices: 18.7 us -> none  [passed_along(): return lax.ppermute(block, axis, route)]
    ppermute x8 -> x0, starting transfers between devices: 18.7 us -> none  [passed_along(): return lax.ppermute(block, axis, route)]
    pallas_call x2 -> x1, Pallas kernels: 72.5 us -> 90.3 us  [image_and_gram(): pl.pallas_call(functools.partial(image_kernel, total), name='image', out_...]
    concatenate x14 -> x1, local copies, waits for them, and re-layouts: 17.2 us -> 0.63 us  [on_device(): inside = jnp.concatenate([inside, jnp.ones_like(inside[:1])], axis=0)]
    unnamed x14 -> x0, local copies, waits for them, and re-layouts: 8.07 us -> none
    another operation x6 -> x0, local copies, waits for them, and re-layouts: 7.56 us -> none
  transfers between devices with their start and end apart: 8 -> 0, of which waited for: 2 -> 0; matrix products, arithmetic and copies ran while one was open for 17% -> 0% of each run, Pallas kernels for 0% -> 0%
where the time goes in v2:
time: 125 us; the launch traced here: 124 us
  Pallas kernels  120 us (96%)
  other arithmetic  3.53 us (3%)
    pallas_call x1, Pallas kernels, image_and_gram(): pl.pallas_call(functools.partial(image_kernel, total), name='image', out_...  90.3 us
    pallas_call x1, Pallas kernels, basis_and_factor(): pl.pallas_call(basis_kernel, name='basis', grid=(rows // step,), out_shap...  29.4 us

profile of v2, /device:TPU:1, one launch (start us, length us, event | category | flops | bytes accessed | tf_op | source)
XLA Modules:
  0.0 124.5 jit_solution(9077620412299581110)
XLA Ops:
  0.6 0.1 pad_add_fusion
  0.7 1.2 divide_multiply_fusion.scale
  1.9 1.3 %fusion.6.cols = s32[32,32]{1,0:T(8,128)} fusion(s32[32,32]{1,0:T(8,128)} %param.6, s32[]{:T(128)S(6)} %axis_index.23), kind=kLoop, calls=%fused_computation.16 | loop fusion | flops 38912 | bytes 8196 | tf_op jit(solution)/shard_map/add | solution.py:429
  3.2 0.9 fusion
  4.2 0.6 concatenate.3
  4.8 90.3 %image.1 = (f32[32,128,128]{2,1,0:T(8,128)}, f32[16,8,128]{2,1,0:T(8,128)}) custom-call(s32[32,32]{1,0:T(8,128)} %fusion.6.cols, f32[3]{0:T(128)} %divide_multiply_fusion.scale, bf16[128,128]{1,0:T(8,128)(2,1)} %bitcast.12, bf16[32,128,128]{2,1,0:T(8,128)(2,1)} %bitcast.11), custom_call_target="tpu_custom_call" | custom-call | tf_op jit(solution)/shard_map/image/pallas_call | solution.py:277
  95.1 29.4 %basis.1 = (f32[4096,128]{1,0:T(8,128)}, f32[128,128]{1,0:T(8,128)}) custom-call(f32[128,128]{1,0:T(8,128)} %bitcast.13, f32[4096,128]{1,0:T(8,128)} %bitcast.10), custom_call_target="tpu_custom_call" | custom-call | tf_op jit(solution)/shard_map/basis/pallas_call | solution.py:391

commit v3 on v2

v3 whole, which is shorter than its diff:
```python
import functools
import math

import jax
import jax.numpy as jnp
from jax import lax
from jax.experimental import pallas as pl
from jax.experimental.pallas import tpu as pltpu
from jax.sharding import PartitionSpec as P

AZ_SEC = 8
DZ = 8
CUTOFF = 3.0
NUGGET = 0.5
BS = 128
LOG2E = 1.4426950408889634
MESH = pl.DeviceIdType.MESH
F32 = jnp.float32
BF16 = jnp.bfloat16
HIGHEST = lax.Precision.HIGHEST


STEPS = 5


def place():
    s = lax.axis_index("sector")
    d = lax.axis_index("depth")
    return s // 4, (s // 2) % 2, s % 2, d // 8, d % 8


def short(value):
    return value.astype(BF16).astype(F32)


def pieces(value):
    one = short(value)
    two = short(value - one)
    return one, two, value - one - two


def image_kernel(
    total, slabs, near, ranges, coords_ref, own_ref, image_ref, gram_ref,
    block_ref, wide_ref, place_ref, mine_ref, point_ref, right_ref, left_ref, local_ref,
    part_ref, got1, got2, got3, got4, one_sum, two_sum, three_sum,
    place_s, place_r, cross_s, cross_r, along_s, along_r, twin_s, twin_r, own_s, own_r,
    s1, r1, s2, r2, s3, r3, s4, r4,
):
    rows, rank = own_ref.shape[0], own_ref.shape[2]
    slots = near.shape[1]
    chunks = cross_s.shape[0]
    size = rows // chunks
    y, xh, core, xl, z = place()
    s = lax.axis_index("sector")
    d = lax.axis_index("depth")
    x = xh * 2 + xl
    a = core * 4 + x

    def sector(k):
        return lax.rem(s + k + 16, 16), d

    def peer_a(k):
        p = lax.rem(a + k, 8)
        px = lax.rem(p, 4)
        return p, (y * 4 + (px // 2) * 2 + p // 4, lax.rem(px, 2) * 8 + z)

    def peer_y(k):
        return lax.rem(s + 4 * k, 16), d

    def peer_z(k):
        return s, xl * 8 + lax.rem(z + k, 8)

    barrier = pltpu.get_barrier_semaphore()
    greeted = [sector(k) for k in (-2, -1, 1, 2)]
    greeted += [peer_y(k) for k in range(1, 4)]
    greeted += [peer_a(k)[1] for k in range(1, 8)] + [peer_z(k) for k in range(1, 8)]
    for device in greeted:
        pl.semaphore_signal(barrier, inc=1, device_id=device, device_id_type=MESH)

    corner = lax.broadcasted_iota(jnp.int32, (3, 1), 0)
    corner = jnp.where(corner == 0, s * AZ_SEC, jnp.where(corner == 1, 32, d * DZ + DZ // 2))
    point_ref[...] = jnp.ones_like(point_ref)
    for g in range(rows):
        inside = coords_ref[:, g * BS : (g + 1) * BS] - corner
        point_ref[4 * g : 4 * g + 3, :] = inside.astype(F32)
    mine_ref[...] = point_ref[...].astype(BF16)

    shift = (slabs * rows).bit_length() - 1

    def column(g, n):
        block = near[g, n]
        step = lax.rem(lax.shift_right_logical(block, shift) - s + 18, 16)
        return jnp.minimum(step, STEPS - 1) * rows + lax.rem(block, rows)

    pl.semaphore_wait(barrier, len(greeted))

    opposite = sector(2 - 4 * xh)
    onward = sector(4 - 8 * xh)
    across_at = (4 - 4 * xh) * rows
    along_at = 4 * xh * rows
    twin = sector(1 - 2 * core)
    twin_from = (4 - 4 * core) * rows
    twin_to = (3 - 2 * core) * rows
    own_to = (1 + 2 * core) * rows

    def remote(src, dst, send, recv, dev):
        return pltpu.make_async_remote_copy(
            src, dst, send, recv, device_id=dev, device_id_type=MESH
        )

    def place_copy(i):
        k = (-2, -1, 1, 2)[i]
        return remote(mine_ref, place_ref.at[2 - k], place_s.at[i], place_r.at[i], sector(k))

    def cross_copy(c):
        return remote(
            own_ref.at[pl.ds(c * size, size)],
            wide_ref.at[pl.ds(4 * xh * rows + c * size, size)],
            cross_s.at[c], cross_r.at[c], opposite,
        )

    def along_copy(c):
        return remote(
            wide_ref.at[pl.ds(across_at + c * size, size)],
            wide_ref.at[pl.ds(along_at + c * size, size)],
            along_s.at[c], along_r.at[c], onward,
        )

    def twin_copy(c):
        return remote(
            wide_ref.at[pl.ds(twin_from + c * size, size)],
            wide_ref.at[pl.ds(twin_to + c * size, size)],
            twin_s.at[c], twin_r.at[c], twin,
        )

    def own_copy():
        return remote(own_ref, wide_ref.at[pl.ds(own_to, rows)], own_s, own_r, twin)

    def every(count, do):
        def step(k, c):
            do(k)
            return c

        lax.fori_loop(0, count, step, 0)

    for i in range(4):
        place_copy(i).start()
    window = 4
    every(window, lambda c: cross_copy(c).start())
    own_copy().start()
    wide_ref[pl.ds(2 * rows, rows)] = own_ref[...]
    local_ref[...] = jnp.zeros_like(local_ref)

    line = lax.broadcasted_iota(jnp.int32, (1, 8, BS), 1)
    w = jnp.where(line == 0, ranges[0], jnp.where(line == 1, ranges[1], ranges[2]))
    w = LOG2E / w
    w = jnp.where(line < 3, w * w, 0.0)

    def spread(ref_value, step):
        even = ref_value.astype(F32).reshape(rows // 2, 8, BS)
        odd = jnp.concatenate([even[:, 4:], even[:, :4]], axis=1)
        both = jnp.stack([even, odd], axis=1).reshape(rows, 8, BS)
        both = both + jnp.where(line == 0, 8.0 * (step - 2) - 4.0, 0.0)
        norm = jnp.sum(both * both * w, axis=1, keepdims=True)
        return both, norm

    def put_right(both, norm, step):
        n1, n2, n3 = pieces(norm)
        tail = jnp.where(line == 4, n1, jnp.where(line == 5, n2, jnp.where(line == 6, n3, 0.0)))
        base = jnp.where(line < 4, both, tail)
        twice = jnp.concatenate([base, base], axis=1).astype(BF16)
        right_ref[pl.ds(step * rows, rows)] = twice

    both, norm = spread(point_ref[...], 2)
    put_right(both, norm, 2)
    full = jnp.where(line < 3, -2.0 * w * both, jnp.where(line == 3, norm, 0.0))
    a1, a2, a3 = pieces(full)
    a1 = a1 + jnp.where(jnp.logical_and(line > 3, line < 7), 1.0, 0.0)
    left_ref[...] = jnp.concatenate([a1, a2, a3, jnp.zeros_like(a1)], axis=1)
    for i in range(4):
        place_copy(i).wait_recv()
    for step in (0, 1, 3, 4):
        both, norm = spread(place_ref[step], step)
        put_right(both, norm, step)

    def build(g):
        left = jnp.transpose(left_ref[g]).astype(BF16)
        for n in range(0, slots, 2):
            right = jnp.concatenate([right_ref[column(g, n)], right_ref[column(g, n + 1)]], axis=1)
            right = jnp.concatenate([right, right], axis=0)
            square = jnp.dot(left, right, preferred_element_type=F32)
            square = jnp.maximum(square, 1e-10)
            rest = CUTOFF * LOG2E - square * lax.rsqrt(square)
            taper = jnp.maximum(rest, 0.0)
            block = jnp.exp2(rest) * taper * taper
            block_ref[g, :, n * BS : (n + 2) * BS] = block.astype(BF16)

    lag = 2

    def turn(c, carry):
        every(size, lambda i: build(c * size + i))
        cross_copy(c).wait_recv()
        along_copy(c).start()

        @pl.when(c + window < chunks)
        def _():
            cross_copy(c + window).start()

        @pl.when(c >= lag)
        def _():
            along_copy(c - lag).wait_recv()
            twin_copy(c - lag).start()

        return carry

    lax.fori_loop(0, chunks, turn, 0)

    def tail(i):
        along_copy(chunks - lag + i).wait_recv()
        twin_copy(chunks - lag + i).start()

    every(lag, tail)
    own_copy().wait_recv()
    every(chunks, lambda c: twin_copy(c).wait_recv())

    factor = math.exp(-CUTOFF) / (8.0 * (CUTOFF * LOG2E) ** 2)

    def multiply(g):
        acc = jnp.zeros((BS, rank), F32)
        for n in range(0, slots, 2):
            parts = jnp.concatenate([wide_ref[column(g, n)], wide_ref[column(g, n + 1)]], axis=0)
            acc = acc + jnp.dot(
                block_ref[g, :, n * BS : (n + 2) * BS], parts, preferred_element_type=F32
            )
        image = acc * factor + NUGGET * own_ref[g].astype(F32)
        image_ref[g] = image
        high = image.astype(BF16)
        low = (image - high.astype(F32)).astype(BF16)
        pair = jnp.concatenate([high, low], axis=1)
        local_ref[...] += lax.dot_general(
            high, pair, (((0,), (0,)), ((), ())), preferred_element_type=F32
        )

    every(rows, multiply)
    cross = local_ref[:, rank:]
    part = local_ref[:, :rank] + cross + jnp.transpose(cross)
    part_ref[...] = part.reshape(part_ref.shape)

    def copy1(k):
        p, device = peer_a(k)
        return remote(part_ref.at[p], got1.at[a], s1.at[k], r1.at[k], device)

    def copy2(k):
        return remote(one_sum, got2.at[y], s2.at[k], r2.at[k], peer_y(k))

    def copy3(k):
        return remote(two_sum, got3.at[z], s3.at[k], r3.at[k], peer_z(k))

    def copy4(k):
        return remote(three_sum, got4.at[a], s4.at[k], r4.at[k], peer_a(k)[1])

    def exchange(copy, count, own, value, got):
        for k in range(1, count):
            copy(k).start()
        got[own] = value
        for k in range(1, count):
            copy(k).wait_recv()

    exchange(copy1, 8, a, part_ref[a], got1)
    one_sum[...] = jnp.sum(got1[...], axis=0)
    exchange(copy2, 4, y, one_sum[...], got2)
    two_sum[...] = jnp.sum(got2[...], axis=0)
    exchange(copy3, 8, z, two_sum[...], got3)
    three_sum[...] = jnp.sum(got3[...], axis=0) * (1.0 / total)
    exchange(copy4, 8, a, three_sum[...], got4)
    gram_ref[...] = got4[...]

    for i in range(4):
        place_copy(i).wait_send()
    own_copy().wait_send()
    every(chunks, lambda c: cross_copy(c).wait_send())
    every(chunks, lambda c: along_copy(c).wait_send())
    every(chunks, lambda c: twin_copy(c).wait_send())
    for copy, count in ((copy1, 8), (copy2, 4), (copy3, 8), (copy4, 8)):
        for k in range(1, count):
            copy(k).wait_send()


def image_and_gram(near, ranges, coords, own, slabs, total):
    rows, size, rank = own.shape
    slots = near.shape[1]
    chunks = 16
    vmem = pl.BlockSpec(memory_space=pltpu.VMEM)
    smem = pl.BlockSpec(memory_space=pltpu.SMEM)
    dma = pltpu.SemaphoreType.DMA
    piece = rank // 8
    image, gram = pl.pallas_call(
        functools.partial(image_kernel, total, slabs),
        name="image",
        out_shape=(
            jax.ShapeDtypeStruct((rows, size, rank), F32),
            jax.ShapeDtypeStruct((8, piece, rank), F32),
        ),
        in_specs=[smem, smem, vmem, vmem],
        out_specs=(vmem, vmem),
        scratch_shapes=[
            pltpu.VMEM((rows, size, slots * size), BF16),
            pltpu.VMEM((STEPS * rows, size, rank), BF16),
            pltpu.VMEM((STEPS, rows * 4, size), BF16),
            pltpu.VMEM((rows * 4, size), BF16),
            pltpu.VMEM((rows * 4, size), F32),
            pltpu.VMEM((STEPS * rows, 16, size), BF16),
            pltpu.VMEM((rows, 32, size), F32),
            pltpu.VMEM((rank, 2 * rank), F32),
        ]
        + [pltpu.VMEM((n, piece, rank), F32) for n in (8, 8, 4, 8, 8)]
        + [pltpu.VMEM((piece, rank), F32)] * 3
        + [dma((4,))] * 2
        + [dma((chunks,))] * 6
        + [dma(())] * 2
        + [dma((n,)) for n in (8, 8, 4, 4, 8, 8, 8, 8)],
        compiler_params=pltpu.CompilerParams(
            collective_id=1, has_side_effects=True, vmem_limit_bytes=58 << 20
        ),
    )(near, ranges, coords, own)
    return image, gram.reshape(rank, rank)


def nt(a, b):
    return lax.dot_general(
        a, b, (((1,), (1,)), ((), ())), precision=HIGHEST, preferred_element_type=F32
    )


def nn(a, b):
    return jnp.dot(a, b, precision=HIGHEST, preferred_element_type=F32)


def basis_kernel(
    gram_ref, image_hbm, basis_hbm, factor_ref, inverse_ref, work_ref, image_ref, out_ref,
    in_sem, out_sem,
):
    n = gram_ref.shape[0]
    chunks = out_sem.shape[0]
    size = image_ref.shape[0] // chunks
    fetch = pltpu.make_async_copy(image_hbm, image_ref, in_sem)
    fetch.start()

    row = lax.broadcasted_iota(jnp.int32, (n, n), 0)
    col = lax.broadcasted_iota(jnp.int32, (n, n), 1)
    diag = row == col
    weight = jnp.where(row > col, 1.0, jnp.where(diag, 0.5, 0.0)).astype(F32)
    eye = jnp.where(diag, 1.0, 0.0).astype(F32)
    gram = gram_ref[...]
    only = jnp.where(diag, gram, 0.0)
    down = lax.rsqrt(jnp.sum(only, axis=1, keepdims=True))
    across = lax.rsqrt(jnp.sum(only, axis=0, keepdims=True))
    first = gram * down * across - eye
    inverse_ref[...] = (eye - first * weight) * across

    def unsettled(state):
        size, turn = state
        return jnp.logical_and(jnp.logical_not(size < 1e-6), turn < 8)

    def refine(state):
        turn = state[1]
        x = inverse_ref[...]
        gap = nt(nn(x, gram_ref[...]), x) - eye
        inverse_ref[...] = x - nn(gap * weight, x)
        return jnp.sum(gap * gap), turn + 1

    far, _ = lax.while_loop(unsettled, refine, (jnp.sum(first * first), jnp.int32(0)))
    settled = far < 1e-6

    @pl.when(settled)
    def _():
        factor_ref[...] = jnp.where(row <= col, nn(inverse_ref[...], gram_ref[...]), 0.0)

    @pl.when(jnp.logical_not(settled))
    def _():
        work_ref[:, :n] = gram_ref[...]
        work_ref[:, n:] = eye
        wide = lax.broadcasted_iota(jnp.int32, (n, 2 * n), 1)
        tall = lax.broadcasted_iota(jnp.int32, (n, 1), 0)

        def eliminate(k, c):
            m = work_ref[...]
            pivot_row = jnp.sum(jnp.where(tall == k, m, 0.0), axis=0, keepdims=True)
            column = jnp.sum(jnp.where(wide == k, m, 0.0), axis=1, keepdims=True)
            pivot = jnp.sum(jnp.where(tall == k, column, 0.0), axis=0, keepdims=True)
            ratio = jnp.where(tall > k, column / pivot, 0.0)
            work_ref[...] = m - ratio * pivot_row
            return c

        lax.fori_loop(0, n, eliminate, 0)
        upper = work_ref[:, :n]
        scale = lax.rsqrt(jnp.sum(jnp.where(diag, upper, 0.0), axis=1, keepdims=True))
        factor_ref[...] = jnp.where(row <= col, upper * scale, 0.0)
        inverse_ref[...] = work_ref[:, n:] * scale

    x = jnp.transpose(inverse_ref[...])
    xh = x.astype(BF16)
    xl = (x - xh.astype(F32)).astype(BF16)
    right = jnp.concatenate(
        [
            jnp.concatenate([xh, xl], axis=1),
            jnp.concatenate([xh, jnp.zeros_like(xl)], axis=1),
        ],
        axis=0,
    )
    fetch.wait()

    def send(i):
        piece = pl.ds(i * size, size)
        return pltpu.make_async_copy(out_ref.at[piece], basis_hbm.at[piece], out_sem.at[i])

    for i in range(chunks):
        image = image_ref[i * size : (i + 1) * size]
        high = image.astype(BF16)
        low = (image - high.astype(F32)).astype(BF16)
        both = jnp.concatenate([high, low], axis=1)
        product = jnp.dot(both, right, preferred_element_type=F32)
        out_ref[i * size : (i + 1) * size] = product[:, :n] + product[:, n:]
        send(i).start()
    for i in range(chunks):
        send(i).wait()


def basis_and_factor(gram, image):
    n = gram.shape[0]
    rows = image.shape[0]
    chunks = 8
    vmem = pl.BlockSpec(memory_space=pltpu.VMEM)
    hbm = pl.BlockSpec(memory_space=pl.ANY)
    return pl.pallas_call(
        basis_kernel,
        name="basis",
        out_shape=(
            jax.ShapeDtypeStruct((rows, n), F32),
            jax.ShapeDtypeStruct((n, n), F32),
        ),
        in_specs=[vmem, hbm],
        out_specs=(hbm, vmem),
        scratch_shapes=[
            pltpu.VMEM((n, n), F32),
            pltpu.VMEM((n, 2 * n), F32),
            pltpu.VMEM((rows, n), F32),
            pltpu.VMEM((rows, n), F32),
            pltpu.SemaphoreType.DMA(()),
            pltpu.SemaphoreType.DMA((chunks,)),
        ],
    )(gram, image)


def on_device(panel, coords, neighbours, ranges):
    block_count = neighbours.shape[0]
    block_size = panel.shape[0] // block_count
    width = panel.shape[1]
    sector_count = lax.axis_size("sector")
    slab_count = lax.axis_size("depth")
    blocked = panel.reshape(block_count, block_size, width)

    total_cells = float(panel.shape[0] * sector_count * slab_count)
    image, gram = image_and_gram(
        neighbours, ranges, coords, blocked, slab_count, total_cells
    )
    image = image.reshape(block_count * block_size, width)
    basis, factor = basis_and_factor(gram, image)
    return (basis, factor)


def solution(mesh):
    in_specs = (
        P(("sector", "depth"), None),
        P(None, ("sector", "depth")),
        P(("sector", "depth"), None),
        P(),
    )
    out_specs = (P(("sector", "depth"), None), P())
    return jax.shard_map(
        on_device, mesh=mesh, in_specs=in_specs, out_specs=out_specs, check_vma=False
    )
```

time: 125 us -> 118 us (0.944)
  other arithmetic: 3.53 us -> 0 us
  Pallas kernels: 120 us -> 117 us
    pallas_call x2, Pallas kernels: 120 us -> 117 us  [the longest x1 90.6 us: image_and_gram(): pl.pallas_call(functools.partial(image_kernel, total, slabs), name='image...]
    add x1 -> x0, other arithmetic: 1.35 us -> none  [on_device(): local_column = step_away * block_count + neighbours % block_count]
where the time goes in v3:
time: 118 us; the launch traced here: 117 us
  Pallas kernels  117 us (99%)
    pallas_call x1, Pallas kernels, image_and_gram(): pl.pallas_call(functools.partial(image_kernel, total, slabs), name='image...  90.6 us
    pallas_call x1, Pallas kernels, basis_and_factor(): pl.pallas_call(basis_kernel, name='basis', out_shape=(jax.ShapeDtypeStruc...  26.1 us

profile of v3, /device:TPU:1, one launch (start us, length us, event | category | flops | bytes accessed | tf_op | source)
XLA Modules:
  0.0 117.4 jit_solution(2149423653776438724)
XLA Ops:
  0.6 90.6 %image.1 = (f32[32,128,128]{2,1,0:T(8,128)}, f32[8,16,128]{2,1,0:T(8,128)}) custom-call(s32[32,32]{1,0:T(8,128)} %near.1, f32[3]{0:T(128)} %ranges.1, s32[3,4096]{1,0:T(4,128)} %coords_ref.1, bf16[32,128,128]{2,1,0:T(8,128)(2,1)} %bitcast.4), custom_call_target="tpu_custom_call" | custom-call | tf_op jit(solution)/shard_map/image/pallas_call | solution.py:297
  91.3 26.1 %basis.1 = (f32[4096,128]{1,0:T(8,128)}, f32[128,128]{1,0:T(8,128)}) custom-call(f32[128,128]{1,0:T(8,128)} %bitcast.5, f32[4096,128]{1,0:T(8,128)} %bitcast.3), custom_call_target="tpu_custom_call" | custom-call | tf_op jit(solution)/shard_map/basis/pallas_call | solution.py:435

commit v4 on v3

--- a/solution.py
+++ b/solution.py
@@ -40,11 +40,11 @@
 
 
 def image_kernel(
-    total, slabs, near, ranges, coords_ref, own_ref, image_ref, gram_ref,
-    block_ref, wide_ref, place_ref, mine_ref, point_ref, right_ref, left_ref, local_ref,
+    total, slabs, near, ranges, coords_ref, own_ref, image_hbm, gram_ref,
+    early_ref, late_ref, image_ref, wide_ref, place_ref, mine_ref, point_ref, right_ref, left_ref, local_ref,
     part_ref, got1, got2, got3, got4, one_sum, two_sum, three_sum,
     place_s, place_r, cross_s, cross_r, along_s, along_r, twin_s, twin_r, own_s, own_r,
-    s1, r1, s2, r2, s3, r3, s4, r4,
+    s1, r1, s2, r2, s3, r3, s4, r4, out_sem,
 ):
     rows, rank = own_ref.shape[0], own_ref.shape[2]
     slots = near.shape[1]
@@ -146,8 +146,7 @@
     for i in range(4):
         place_copy(i).start()
     window = 4
-    every(window, lambda c: cross_copy(c).start())
-    own_copy().start()
+    cross_copy(0).start()
     wide_ref[pl.ds(2 * rows, rows)] = own_ref[...]
     local_ref[...] = jnp.zeros_like(local_ref)
 
@@ -179,26 +178,42 @@
     left_ref[...] = jnp.concatenate([a1, a2, a3, jnp.zeros_like(a1)], axis=1)
     for i in range(4):
         place_copy(i).wait_recv()
+    for c in range(1, window):
+        cross_copy(c).start()
+    own_copy().start()
     for step in (0, 1, 3, 4):
         both, norm = spread(place_ref[step], step)
         put_right(both, norm, step)
 
+    def left_of(g):
+        return jnp.transpose(left_ref[g]).astype(BF16)
+
+    def block_pair(left, g, n):
+        right = jnp.concatenate([right_ref[column(g, n)], right_ref[column(g, n + 1)]], axis=1)
+        right = jnp.concatenate([right, right], axis=0)
+        square = jnp.dot(left, right, preferred_element_type=F32)
+        square = jnp.maximum(square, 1e-10)
+        rest = CUTOFF * LOG2E - square * lax.rsqrt(square)
+        taper = jnp.maximum(rest, 0.0)
+        return (jnp.exp2(rest) * taper * taper).astype(BF16)
+
     def build(g):
-        left = jnp.transpose(left_ref[g]).astype(BF16)
+        left = left_of(g)
         for n in range(0, slots, 2):
-            right = jnp.concatenate([right_ref[column(g, n)], right_ref[column(g, n + 1)]], axis=1)
-            right = jnp.concatenate([right, right], axis=0)
-            square = jnp.dot(left, right, preferred_element_type=F32)
-            square = jnp.maximum(square, 1e-10)
-            rest = CUTOFF * LOG2E - square * lax.rsqrt(square)
-            taper = jnp.maximum(rest, 0.0)
-            block = jnp.exp2(rest) * taper * taper
-            block_ref[g, :, n * BS : (n + 2) * BS] = block.astype(BF16)
-
+            early_ref[g, :, n * BS : (n + 2) * BS] = block_pair(left, g, n)
+
+    early = early_ref.shape[0]
+    late = late_ref.shape[0]
+    share = early // late
+    paced = early - 2
     lag = 2
 
     def turn(c, carry):
-        every(size, lambda i: build(c * size + i))
+        def row(g, carry):
+            build(g)
+            return carry
+
+        lax.fori_loop((c * paced) // chunks, ((c + 1) * paced) // chunks, row, 0)
         cross_copy(c).wait_recv()
         along_copy(c).start()
 
@@ -214,6 +229,8 @@
         return carry
 
     lax.fori_loop(0, chunks, turn, 0)
+    for g in range(paced, early):
+        build(g)
 
     def tail(i):
         along_copy(chunks - lag + i).wait_recv()
@@ -225,15 +242,20 @@
 
     factor = math.exp(-CUTOFF) / (8.0 * (CUTOFF * LOG2E) ** 2)
 
-    def multiply(g):
+    def out_copy(g):
+        return pltpu.make_async_copy(image_ref.at[g], image_hbm.at[g], out_sem.at[g])
+
+    def multiply(g, source, at, beside):
         acc = jnp.zeros((BS, rank), F32)
         for n in range(0, slots, 2):
             parts = jnp.concatenate([wide_ref[column(g, n)], wide_ref[column(g, n + 1)]], axis=0)
+            beside()
             acc = acc + jnp.dot(
-                block_ref[g, :, n * BS : (n + 2) * BS], parts, preferred_element_type=F32
+                source[at, :, n * BS : (n + 2) * BS], parts, preferred_element_type=F32
             )
         image = acc * factor + NUGGET * own_ref[g].astype(F32)
         image_ref[g] = image
+        out_copy(g).start()
         high = image.astype(BF16)
         low = (image - high.astype(F32)).astype(BF16)
         pair = jnp.concatenate([high, low], axis=1)
@@ -241,7 +263,23 @@
             high, pair, (((0,), (0,)), ((), ())), preferred_element_type=F32
         )
 
-    every(rows, multiply)
+    def both_at_once(t):
+        left = left_of(early + t)
+        done = [0, 0]
+
+        def beside():
+            if done[0] % share == 0:
+                n = 2 * done[1]
+                late_ref[t, :, n * BS : (n + 2) * BS] = block_pair(left, early + t, n)
+                done[1] += 1
+            done[0] += 1
+
+        for i in range(share):
+            g = t * share + i
+            multiply(g, early_ref, g, beside)
+
+    every(late, both_at_once)
+    every(late, lambda t: multiply(early + t, late_ref, t, lambda: None))
     cross = local_ref[:, rank:]
     part = local_ref[:, :rank] + cross + jnp.transpose(cross)
     part_ref[...] = part.reshape(part_ref.shape)
@@ -275,6 +313,7 @@
     exchange(copy4, 8, a, three_sum[...], got4)
     gram_ref[...] = got4[...]
 
+    every(rows, lambda g: out_copy(g).wait())
     for i in range(4):
         place_copy(i).wait_send()
     own_copy().wait_send()
@@ -290,6 +329,8 @@
     rows, size, rank = own.shape
     slots = near.shape[1]
     chunks = 16
+    late = rows // 8
+    early = rows - late
     vmem = pl.BlockSpec(memory_space=pltpu.VMEM)
     smem = pl.BlockSpec(memory_space=pltpu.SMEM)
     dma = pltpu.SemaphoreType.DMA
@@ -302,9 +343,11 @@
             jax.ShapeDtypeStruct((8, piece, rank), F32),
         ),
         in_specs=[smem, smem, vmem, vmem],
-        out_specs=(vmem, vmem),
+        out_specs=(pl.BlockSpec(memory_space=pl.ANY), vmem),
         scratch_shapes=[
-            pltpu.VMEM((rows, size, slots * size), BF16),
+            pltpu.VMEM((early, size, slots * size), BF16),
+            pltpu.VMEM((late, size, slots * size), BF16),
+            pltpu.VMEM((rows, size, rank), F32),
             pltpu.VMEM((STEPS * rows, size, rank), BF16),
             pltpu.VMEM((STEPS, rows * 4, size), BF16),
             pltpu.VMEM((rows * 4, size), BF16),
@@ -318,7 +361,7 @@
         + [dma((4,))] * 2
         + [dma((chunks,))] * 6
         + [dma(())] * 2
-        + [dma((n,)) for n in (8, 8, 4, 4, 8, 8, 8, 8)],
+        + [dma((n,)) for n in (8, 8, 4, 4, 8, 8, 8, 8, rows)],
         compiler_params=pltpu.CompilerParams(
             collective_id=1, has_side_effects=True, vmem_limit_bytes=58 << 20
         ),

time: 118 us -> 114 us (0.966)
  Pallas kernels: 117 us -> 113 us
    pallas_call x1, Pallas kernels: 90.6 us -> 86.9 us  [image_and_gram(): pl.pallas_call(functools.partial(image_kernel, total, slabs), name='image...]
where the time goes in v4:
time: 114 us
  Pallas kernels  113 us (99%)
    pallas_call x1, Pallas kernels, image_and_gram(): pl.pallas_call(functools.partial(image_kernel, total, slabs), name='image...  86.9 us
    pallas_call x1, Pallas kernels, basis_and_factor(): pl.pallas_call(basis_kernel, name='basis', out_shape=(jax.ShapeDtypeStruc...  26.1 us

profile of v4, /device:TPU:1, one launch (start us, length us, event | category | flops | bytes accessed | tf_op | source)
XLA Modules:
  0.0 113.7 jit_solution(10060461435733397726)
XLA Ops:
  0.6 86.9 %image.1 = (f32[32,128,128]{2,1,0:T(8,128)}, f32[8,16,128]{2,1,0:T(8,128)}) custom-call(s32[32,32]{1,0:T(8,128)} %near.1, f32[3]{0:T(128)} %ranges.1, s32[3,4096]{1,0:T(4,128)} %coords_ref.1, bf16[32,128,128]{2,1,0:T(8,128)(2,1)} %bitcast.4), custom_call_target="tpu_custom_call" | custom-call | tf_op jit(solution)/shard_map/image/pallas_call | solution.py:338
  87.5 26.1 %basis.1 = (f32[4096,128]{1,0:T(8,128)}, f32[128,128]{1,0:T(8,128)}) custom-call(f32[128,128]{1,0:T(8,128)} %bitcast.5, f32[4096,128]{1,0:T(8,128)} %bitcast.3), custom_call_target="tpu_custom_call" | custom-call | tf_op jit(solution)/shard_map/basis/pallas_call | solution.py:478

commit v5 on v4

--- a/solution.py
+++ b/solution.py
@@ -48,7 +48,7 @@
 ):
     rows, rank = own_ref.shape[0], own_ref.shape[2]
     slots = near.shape[1]
-    chunks = cross_s.shape[0]
+    chunks = cross_r.shape[0]
     size = rows // chunks
     y, xh, core, xl, z = place()
     s = lax.axis_index("sector")
@@ -110,27 +110,35 @@
 
     def place_copy(i):
         k = (-2, -1, 1, 2)[i]
-        return remote(mine_ref, place_ref.at[2 - k], place_s.at[i], place_r.at[i], sector(k))
+        return remote(mine_ref, place_ref.at[2 - k], place_s, place_r, sector(k))
+
+    def all_places():
+        four = place_ref.at[pl.ds(0, 4)]
+        return remote(four, four, place_s, place_r, twin)
+
+    def all_rows(send, recv):
+        whole = wide_ref.at[pl.ds(0, rows)]
+        return remote(whole, whole, send, recv, twin)
 
     def cross_copy(c):
         return remote(
             own_ref.at[pl.ds(c * size, size)],
             wide_ref.at[pl.ds(4 * xh * rows + c * size, size)],
-            cross_s.at[c], cross_r.at[c], opposite,
+            cross_s, cross_r.at[c], opposite,
         )
 
     def along_copy(c):
         return remote(
             wide_ref.at[pl.ds(across_at + c * size, size)],
             wide_ref.at[pl.ds(along_at + c * size, size)],
-            along_s.at[c], along_r.at[c], onward,
+            along_s, along_r.at[c], onward,
         )
 
     def twin_copy(c):
         return remote(
             wide_ref.at[pl.ds(twin_from + c * size, size)],
             wide_ref.at[pl.ds(twin_to + c * size, size)],
-            twin_s.at[c], twin_r.at[c], twin,
+            twin_s, twin_r, twin,
         )
 
     def own_copy():
@@ -145,10 +153,12 @@
 
     for i in range(4):
         place_copy(i).start()
-    window = 4
-    cross_copy(0).start()
+    for c in range(chunks):
+        cross_copy(c).start()
+    own_copy().start()
     wide_ref[pl.ds(2 * rows, rows)] = own_ref[...]
     local_ref[...] = jnp.zeros_like(local_ref)
+    image_ref[0] = jnp.zeros((BS, rank), F32)
 
     line = lax.broadcasted_iota(jnp.int32, (1, 8, BS), 1)
     w = jnp.where(line == 0, ranges[0], jnp.where(line == 1, ranges[1], ranges[2]))
@@ -176,11 +186,7 @@
     a1, a2, a3 = pieces(full)
     a1 = a1 + jnp.where(jnp.logical_and(line > 3, line < 7), 1.0, 0.0)
     left_ref[...] = jnp.concatenate([a1, a2, a3, jnp.zeros_like(a1)], axis=1)
-    for i in range(4):
-        place_copy(i).wait_recv()
-    for c in range(1, window):
-        cross_copy(c).start()
-    own_copy().start()
+    all_places().wait_recv()
     for step in (0, 1, 3, 4):
         both, norm = spread(place_ref[step], step)
         put_right(both, norm, step)
@@ -205,8 +211,8 @@
     early = early_ref.shape[0]
     late = late_ref.shape[0]
     share = early // late
-    paced = early - 2
     lag = 2
+    paced = early - 2 * lag
 
     def turn(c, carry):
         def row(g, carry):
@@ -217,10 +223,6 @@
         cross_copy(c).wait_recv()
         along_copy(c).start()
 
-        @pl.when(c + window < chunks)
-        def _():
-            cross_copy(c + window).start()
-
         @pl.when(c >= lag)
         def _():
             along_copy(c - lag).wait_recv()
@@ -229,23 +231,31 @@
         return carry
 
     lax.fori_loop(0, chunks, turn, 0)
-    for g in range(paced, early):
-        build(g)
 
     def tail(i):
+        every(2, lambda j: build(paced + 2 * i + j))
         along_copy(chunks - lag + i).wait_recv()
         twin_copy(chunks - lag + i).start()
 
     every(lag, tail)
     own_copy().wait_recv()
-    every(chunks, lambda c: twin_copy(c).wait_recv())
+    all_rows(twin_s, twin_r).wait_recv()
 
     factor = math.exp(-CUTOFF) / (8.0 * (CUTOFF * LOG2E) ** 2)
 
     def out_copy(g):
-        return pltpu.make_async_copy(image_ref.at[g], image_hbm.at[g], out_sem.at[g])
+        return pltpu.make_async_copy(image_ref.at[g + 1], image_hbm.at[g], out_sem)
+
+    def add_gram(image):
+        high = image.astype(BF16)
+        low = (image - high.astype(F32)).astype(BF16)
+        pair = jnp.concatenate([high, low], axis=1)
+        local_ref[...] += lax.dot_general(
+            high, pair, (((0,), (0,)), ((), ())), preferred_element_type=F32
+        )
 
     def multiply(g, source, at, beside):
+        add_gram(image_ref[g])
         acc = jnp.zeros((BS, rank), F32)
         for n in range(0, slots, 2):
             parts = jnp.concatenate([wide_ref[column(g, n)], wide_ref[column(g, n + 1)]], axis=0)
@@ -254,14 +264,8 @@
                 source[at, :, n * BS : (n + 2) * BS], parts, preferred_element_type=F32
             )
         image = acc * factor + NUGGET * own_ref[g].astype(F32)
-        image_ref[g] = image
+        image_ref[g + 1] = image
         out_copy(g).start()
-        high = image.astype(BF16)
-        low = (image - high.astype(F32)).astype(BF16)
-        pair = jnp.concatenate([high, low], axis=1)
-        local_ref[...] += lax.dot_general(
-            high, pair, (((0,), (0,)), ((), ())), preferred_element_type=F32
-        )
 
     def both_at_once(t):
         left = left_of(early + t)
@@ -280,56 +284,59 @@
 
     every(late, both_at_once)
     every(late, lambda t: multiply(early + t, late_ref, t, lambda: None))
+    add_gram(image_ref[rows])
     cross = local_ref[:, rank:]
     part = local_ref[:, :rank] + cross + jnp.transpose(cross)
     part_ref[...] = part.reshape(part_ref.shape)
 
     def copy1(k):
         p, device = peer_a(k)
-        return remote(part_ref.at[p], got1.at[a], s1.at[k], r1.at[k], device)
+        return remote(part_ref.at[p], got1.at[a], s1, r1, device)
 
     def copy2(k):
-        return remote(one_sum, got2.at[y], s2.at[k], r2.at[k], peer_y(k))
+        return remote(one_sum, got2.at[y], s2, r2, peer_y(k))
 
     def copy3(k):
-        return remote(two_sum, got3.at[z], s3.at[k], r3.at[k], peer_z(k))
+        return remote(two_sum, got3.at[z], s3, r3, peer_z(k))
 
     def copy4(k):
-        return remote(three_sum, got4.at[a], s4.at[k], r4.at[k], peer_a(k)[1])
-
-    def exchange(copy, count, own, value, got):
+        return remote(three_sum, got4.at[a], s4, r4, peer_a(k)[1])
+
+    def all_pieces(got, count, send, recv):
+        pieces_of_others = got.at[pl.ds(0, count - 1)]
+        return remote(pieces_of_others, pieces_of_others, send, recv, twin)
+
+    def exchange(copy, count, own, value, got, send, recv):
         for k in range(1, count):
             copy(k).start()
         got[own] = value
-        for k in range(1, count):
-            copy(k).wait_recv()
-
-    exchange(copy1, 8, a, part_ref[a], got1)
+        all_pieces(got, count, send, recv).wait_recv()
+
+    exchange(copy1, 8, a, part_ref[a], got1, s1, r1)
     one_sum[...] = jnp.sum(got1[...], axis=0)
-    exchange(copy2, 4, y, one_sum[...], got2)
+    exchange(copy2, 4, y, one_sum[...], got2, s2, r2)
     two_sum[...] = jnp.sum(got2[...], axis=0)
-    exchange(copy3, 8, z, two_sum[...], got3)
+    exchange(copy3, 8, z, two_sum[...], got3, s3, r3)
     three_sum[...] = jnp.sum(got3[...], axis=0) * (1.0 / total)
-    exchange(copy4, 8, a, three_sum[...], got4)
+    exchange(copy4, 8, a, three_sum[...], got4, s4, r4)
     gram_ref[...] = got4[...]
 
-    every(rows, lambda g: out_copy(g).wait())
-    for i in range(4):
-        place_copy(i).wait_send()
+    pltpu.make_async_copy(image_ref.at[pl.ds(1, rows)], image_hbm, out_sem).wait()
+    all_places().wait_send()
     own_copy().wait_send()
-    every(chunks, lambda c: cross_copy(c).wait_send())
-    every(chunks, lambda c: along_copy(c).wait_send())
-    every(chunks, lambda c: twin_copy(c).wait_send())
-    for copy, count in ((copy1, 8), (copy2, 4), (copy3, 8), (copy4, 8)):
-        for k in range(1, count):
-            copy(k).wait_send()
+    for send in (cross_s, along_s, twin_s):
+        all_rows(send, own_r).wait_send()
+    for got, count, send, recv in (
+        (got1, 8, s1, r1), (got2, 4, s2, r2), (got3, 8, s3, r3), (got4, 8, s4, r4),
+    ):
+        all_pieces(got, count, send, recv).wait_send()
 
 
 def image_and_gram(near, ranges, coords, own, slabs, total):
     rows, size, rank = own.shape
     slots = near.shape[1]
-    chunks = 16
-    late = rows // 8
+    chunks = 8
+    late = rows // 4
     early = rows - late
     vmem = pl.BlockSpec(memory_space=pltpu.VMEM)
     smem = pl.BlockSpec(memory_space=pltpu.SMEM)
@@ -347,7 +354,7 @@
         scratch_shapes=[
             pltpu.VMEM((early, size, slots * size), BF16),
             pltpu.VMEM((late, size, slots * size), BF16),
-            pltpu.VMEM((rows, size, rank), F32),
+            pltpu.VMEM((rows + 1, size, rank), F32),
             pltpu.VMEM((STEPS * rows, size, rank), BF16),
             pltpu.VMEM((STEPS, rows * 4, size), BF16),
             pltpu.VMEM((rows * 4, size), BF16),
@@ -358,10 +365,10 @@
         ]
         + [pltpu.VMEM((n, piece, rank), F32) for n in (8, 8, 4, 8, 8)]
         + [pltpu.VMEM((piece, rank), F32)] * 3
-        + [dma((4,))] * 2
-        + [dma((chunks,))] * 6
         + [dma(())] * 2
-        + [dma((n,)) for n in (8, 8, 4, 4, 8, 8, 8, 8, rows)],
+        + [dma(()), dma((chunks,))] * 2
+        + [dma(())] * 12
+        + [dma(())],
         compiler_params=pltpu.CompilerParams(
             collective_id=1, has_side_effects=True, vmem_limit_bytes=58 << 20
         ),

time: 114 us -> 106 us (0.930)
  Pallas kernels: 113 us -> 105 us
    pallas_call x1, Pallas kernels: 86.9 us -> 79.4 us  [image_and_gram(): pl.pallas_call(functools.partial(image_kernel, total, slabs), name='image...]
where the time goes in v5:
time: 106 us
  Pallas kernels  105 us (99%)
    pallas_call x1, Pallas kernels, image_and_gram(): pl.pallas_call(functools.partial(image_kernel, total, slabs), name='image...  79.4 us
    pallas_call x1, Pallas kernels, basis_and_factor(): pl.pallas_call(basis_kernel, name='basis', out_shape=(jax.ShapeDtypeStruc...  26.1 us

profile of v5, /device:TPU:1, one launch (start us, length us, event | category | flops | bytes accessed | tf_op | source)
XLA Modules:
  0.0 106.1 jit_solution(13046148719443766405)
XLA Ops:
  0.6 79.4 %image.1 = (f32[32,128,128]{2,1,0:T(8,128)}, f32[8,16,128]{2,1,0:T(8,128)}) custom-call(s32[32,32]{1,0:T(8,128)} %near.1, f32[3]{0:T(128)} %ranges.1, s32[3,4096]{1,0:T(4,128)} %coords_ref.1, bf16[32,128,128]{2,1,0:T(8,128)(2,1)} %bitcast.4), custom_call_target="tpu_custom_call" | custom-call | tf_op jit(solution)/shard_map/image/pallas_call | solution.py:345
  80.0 26.1 %basis.1 = (f32[4096,128]{1,0:T(8,128)}, f32[128,128]{1,0:T(8,128)}) custom-call(f32[128,128]{1,0:T(8,128)} %bitcast.5, f32[4096,128]{1,0:T(8,128)} %bitcast.3), custom_call_target="tpu_custom_call" | custom-call | tf_op jit(solution)/shard_map/basis/pallas_call | solution.py:485

commit v6 on v5

--- a/solution.py
+++ b/solution.py
@@ -44,12 +44,13 @@
     early_ref, late_ref, image_ref, wide_ref, place_ref, mine_ref, point_ref, right_ref, left_ref, local_ref,
     part_ref, got1, got2, got3, got4, one_sum, two_sum, three_sum,
     place_s, place_r, cross_s, cross_r, along_s, along_r, twin_s, twin_r, own_s, own_r,
-    s1, r1, s2, r2, s3, r3, s4, r4, out_sem,
+    s1, r1, s2, r2, s3, r3, s4, r4, out_sem, own_in_sem,
 ):
     rows, rank = own_ref.shape[0], own_ref.shape[2]
     slots = near.shape[1]
-    chunks = cross_r.shape[0]
-    size = rows // chunks
+    size = rows // 8
+    main = 7
+    ends = [(7 * size, size // 2), (7 * size + size // 2, size // 4), (8 * size - size // 4, size // 4)]
     y, xh, core, xl, z = place()
     s = lax.axis_index("sector")
     d = lax.axis_index("depth")
@@ -108,38 +109,56 @@
             src, dst, send, recv, device_id=dev, device_id_type=MESH
         )
 
-    def place_copy(i):
-        k = (-2, -1, 1, 2)[i]
-        return remote(mine_ref, place_ref.at[2 - k], place_s, place_r, sector(k))
-
-    def all_places():
-        four = place_ref.at[pl.ds(0, 4)]
-        return remote(four, four, place_s, place_r, twin)
+    def place_cross():
+        return remote(mine_ref, place_ref.at[4 * xh], place_s.at[0], place_r.at[0], opposite)
+
+    def place_along():
+        return remote(
+            place_ref.at[4 - 4 * xh], place_ref.at[4 * xh], place_s.at[1], place_r.at[1], onward
+        )
+
+    def place_own():
+        return remote(mine_ref, place_ref.at[1 + 2 * core], place_s.at[2], place_r.at[2], twin)
+
+    def place_twin():
+        return remote(
+            place_ref.at[4 - 4 * core], place_ref.at[3 - 2 * core],
+            place_s.at[3], place_r.at[3], twin,
+        )
 
     def all_rows(send, recv):
         whole = wide_ref.at[pl.ds(0, rows)]
         return remote(whole, whole, send, recv, twin)
 
+    def span(c):
+        return (c * size, size) if not isinstance(c, int) or c < main else ends[c - main]
+
     def cross_copy(c):
+        start, count = span(c)
         return remote(
-            own_ref.at[pl.ds(c * size, size)],
-            wide_ref.at[pl.ds(4 * xh * rows + c * size, size)],
+            own_ref.at[pl.ds(start, count)],
+            wide_ref.at[pl.ds(4 * xh * rows + start, count)],
             cross_s, cross_r.at[c], opposite,
         )
 
     def along_copy(c):
+        start, count = span(c)
         return remote(
-            wide_ref.at[pl.ds(across_at + c * size, size)],
-            wide_ref.at[pl.ds(along_at + c * size, size)],
+            wide_ref.at[pl.ds(across_at + start, count)],
+            wide_ref.at[pl.ds(along_at + start, count)],
             along_s, along_r.at[c], onward,
         )
 
     def twin_copy(c):
+        start, count = span(c)
         return remote(
-            wide_ref.at[pl.ds(twin_from + c * size, size)],
-            wide_ref.at[pl.ds(twin_to + c * size, size)],
+            wide_ref.at[pl.ds(twin_from + start, count)],
+            wide_ref.at[pl.ds(twin_to + start, count)],
             twin_s, twin_r, twin,
         )
+
+    def own_in():
+        return pltpu.make_async_copy(own_ref, wide_ref.at[pl.ds(2 * rows, rows)], own_in_sem)
 
     def own_copy():
         return remote(own_ref, wide_ref.at[pl.ds(own_to, rows)], own_s, own_r, twin)
@@ -151,12 +170,11 @@
 
         lax.fori_loop(0, count, step, 0)
 
-    for i in range(4):
-        place_copy(i).start()
-    for c in range(chunks):
+    place_cross().start()
+    place_own().start()
+    for c in range(main + len(ends)):
         cross_copy(c).start()
-    own_copy().start()
-    wide_ref[pl.ds(2 * rows, rows)] = own_ref[...]
+    own_in().start()
     local_ref[...] = jnp.zeros_like(local_ref)
     image_ref[0] = jnp.zeros((BS, rank), F32)
 
@@ -186,7 +204,13 @@
     a1, a2, a3 = pieces(full)
     a1 = a1 + jnp.where(jnp.logical_and(line > 3, line < 7), 1.0, 0.0)
     left_ref[...] = jnp.concatenate([a1, a2, a3, jnp.zeros_like(a1)], axis=1)
-    all_places().wait_recv()
+    place_cross().wait_recv()
+    place_along().start()
+    place_along().wait_recv()
+    place_twin().start()
+    own_copy().start()
+    place_own().wait_recv()
+    place_twin().wait_recv()
     for step in (0, 1, 3, 4):
         both, norm = spread(place_ref[step], step)
         put_right(both, norm, step)
@@ -212,14 +236,14 @@
     late = late_ref.shape[0]
     share = early // late
     lag = 2
-    paced = early - 2 * lag
+    paced = early - 5
 
     def turn(c, carry):
         def row(g, carry):
             build(g)
             return carry
 
-        lax.fori_loop((c * paced) // chunks, ((c + 1) * paced) // chunks, row, 0)
+        lax.fori_loop((c * paced) // main, ((c + 1) * paced) // main, row, 0)
         cross_copy(c).wait_recv()
         along_copy(c).start()
 
@@ -230,14 +254,22 @@
 
         return carry
 
-    lax.fori_loop(0, chunks, turn, 0)
-
-    def tail(i):
-        every(2, lambda j: build(paced + 2 * i + j))
-        along_copy(chunks - lag + i).wait_recv()
-        twin_copy(chunks - lag + i).start()
-
-    every(lag, tail)
+    lax.fori_loop(0, main, turn, 0)
+
+    def onto_twin(c):
+        along_copy(c).wait_recv()
+        twin_copy(c).start()
+
+    for i in range(len(ends)):
+        build(paced + i)
+        cross_copy(main + i).wait_recv()
+        along_copy(main + i).start()
+        if i < lag:
+            onto_twin(main - lag + i)
+    every(2, lambda j: build(paced + 3 + j))
+    for i in range(len(ends)):
+        onto_twin(main + i)
+    own_in().wait()
     own_copy().wait_recv()
     all_rows(twin_s, twin_r).wait_recv()
 
@@ -263,7 +295,7 @@
             acc = acc + jnp.dot(
                 source[at, :, n * BS : (n + 2) * BS], parts, preferred_element_type=F32
             )
-        image = acc * factor + NUGGET * own_ref[g].astype(F32)
+        image = acc * factor + NUGGET * wide_ref[2 * rows + g].astype(F32)
         image_ref[g + 1] = image
         out_copy(g).start()
 
@@ -322,7 +354,8 @@
     gram_ref[...] = got4[...]
 
     pltpu.make_async_copy(image_ref.at[pl.ds(1, rows)], image_hbm, out_sem).wait()
-    all_places().wait_send()
+    for copy in (place_cross, place_along, place_own, place_twin):
+        copy().wait_send()
     own_copy().wait_send()
     for send in (cross_s, along_s, twin_s):
         all_rows(send, own_r).wait_send()
@@ -335,7 +368,6 @@
 def image_and_gram(near, ranges, coords, own, slabs, total):
     rows, size, rank = own.shape
     slots = near.shape[1]
-    chunks = 8
     late = rows // 4
     early = rows - late
     vmem = pl.BlockSpec(memory_space=pltpu.VMEM)
@@ -349,7 +381,7 @@
             jax.ShapeDtypeStruct((rows, size, rank), F32),
             jax.ShapeDtypeStruct((8, piece, rank), F32),
         ),
-        in_specs=[smem, smem, vmem, vmem],
+        in_specs=[smem, smem, vmem, pl.BlockSpec(memory_space=pl.ANY)],
         out_specs=(pl.BlockSpec(memory_space=pl.ANY), vmem),
         scratch_shapes=[
             pltpu.VMEM((early, size, slots * size), BF16),
@@ -365,10 +397,9 @@
         ]
         + [pltpu.VMEM((n, piece, rank), F32) for n in (8, 8, 4, 8, 8)]
         + [pltpu.VMEM((piece, rank), F32)] * 3
-        + [dma(())] * 2
-        + [dma(()), dma((chunks,))] * 2
-        + [dma(())] * 12
-        + [dma(())],
+        + [dma((4,))] * 2
+        + [dma(()), dma((10,))] * 2
+        + [dma(())] * 14,
         compiler_params=pltpu.CompilerParams(
             collective_id=1, has_side_effects=True, vmem_limit_bytes=58 << 20
         ),

time: 106 us -> 109 us (1.028)
  Pallas kernels: 105 us -> 108 us
    pallas_call x1, Pallas kernels: 79.4 us -> 82 us  [image_and_gram(): pl.pallas_call(functools.partial(image_kernel, total, slabs), name='image...]
where the time goes in v6:
time: 109 us
  Pallas kernels  108 us (99%)
    pallas_call x1, Pallas kernels, image_and_gram(): pl.pallas_call(functools.partial(image_kernel, total, slabs), name='image...  82 us
    pallas_call x1, Pallas kernels, basis_and_factor(): pl.pallas_call(basis_kernel, name='basis', out_shape=(jax.ShapeDtypeStruc...  26.1 us

profile of v6, /device:TPU:1, one launch (start us, length us, event | category | flops | bytes accessed | tf_op | source)
XLA Modules:
  0.0 108.8 jit_solution(3954972200666982826)
XLA Ops:
  0.6 82.0 %image.1 = (f32[32,128,128]{2,1,0:T(8,128)}, f32[8,16,128]{2,1,0:T(8,128)}) custom-call(s32[32,32]{1,0:T(8,128)} %near.1, f32[3]{0:T(128)} %ranges.1, s32[3,4096]{1,0:T(4,128)} %coords_ref.1, bf16[32,128,128]{2,1,0:T(8,128)(2,1)} %bitcast.4), custom_call_target="tpu_custom_call" | custom-call | tf_op jit(solution)/shard_map/image/pallas_call | solution.py:377
  82.7 26.1 %basis.1 = (f32[4096,128]{1,0:T(8,128)}, f32[128,128]{1,0:T(8,128)}) custom-call(f32[128,128]{1,0:T(8,128)} %bitcast.5, f32[4096,128]{1,0:T(8,128)} %bitcast.3), custom_call_target="tpu_custom_call" | custom-call | tf_op jit(solution)/shard_map/basis/pallas_call | solution.py:516

commit v7 on v5

--- a/solution.py
+++ b/solution.py
@@ -48,8 +48,11 @@
 ):
     rows, rank = own_ref.shape[0], own_ref.shape[2]
     slots = near.shape[1]
-    chunks = cross_r.shape[0]
-    size = rows // chunks
+    size = rows // 8
+    half = size // 2
+    main = 6
+    first, last = main, main + 2
+    spans = {first: 0, first + 1: half, last: rows - size, last + 1: rows - half}
     y, xh, core, xl, z = place()
     s = lax.axis_index("sector")
     d = lax.axis_index("depth")
@@ -120,24 +123,30 @@
         whole = wide_ref.at[pl.ds(0, rows)]
         return remote(whole, whole, send, recv, twin)
 
+    def span(c):
+        return (spans[c], half) if isinstance(c, int) and c >= main else (size + c * size, size)
+
     def cross_copy(c):
+        start, count = span(c)
         return remote(
-            own_ref.at[pl.ds(c * size, size)],
-            wide_ref.at[pl.ds(4 * xh * rows + c * size, size)],
+            own_ref.at[pl.ds(start, count)],
+            wide_ref.at[pl.ds(4 * xh * rows + start, count)],
             cross_s, cross_r.at[c], opposite,
         )
 
     def along_copy(c):
+        start, count = span(c)
         return remote(
-            wide_ref.at[pl.ds(across_at + c * size, size)],
-            wide_ref.at[pl.ds(along_at + c * size, size)],
+            wide_ref.at[pl.ds(across_at + start, count)],
+            wide_ref.at[pl.ds(along_at + start, count)],
             along_s, along_r.at[c], onward,
         )
 
     def twin_copy(c):
+        start, count = span(c)
         return remote(
-            wide_ref.at[pl.ds(twin_from + c * size, size)],
-            wide_ref.at[pl.ds(twin_to + c * size, size)],
+            wide_ref.at[pl.ds(twin_from + start, count)],
+            wide_ref.at[pl.ds(twin_to + start, count)],
             twin_s, twin_r, twin,
         )
 
@@ -153,7 +162,7 @@
 
     for i in range(4):
         place_copy(i).start()
-    for c in range(chunks):
+    for c in (first, first + 1, *range(main), last, last + 1):
         cross_copy(c).start()
     own_copy().start()
     wide_ref[pl.ds(2 * rows, rows)] = own_ref[...]
@@ -187,6 +196,17 @@
     a1 = a1 + jnp.where(jnp.logical_and(line > 3, line < 7), 1.0, 0.0)
     left_ref[...] = jnp.concatenate([a1, a2, a3, jnp.zeros_like(a1)], axis=1)
     all_places().wait_recv()
+
+    def onto_next(c):
+        cross_copy(c).wait_recv()
+        along_copy(c).start()
+
+    def onto_twin(c):
+        along_copy(c).wait_recv()
+        twin_copy(c).start()
+
+    onto_next(first)
+    onto_next(first + 1)
     for step in (0, 1, 3, 4):
         both, norm = spread(place_ref[step], step)
         put_right(both, norm, step)
@@ -211,33 +231,40 @@
     early = early_ref.shape[0]
     late = late_ref.shape[0]
     share = early // late
-    lag = 2
-    paced = early - 2 * lag
+    paced = early - 5
+
+    def upto(c):
+        return (7 * c - 3 * ((c + 5) // 6)) // 2
+
+    assert upto(0) == 0 and upto(main) == paced
 
     def turn(c, carry):
         def row(g, carry):
             build(g)
             return carry
 
-        lax.fori_loop((c * paced) // chunks, ((c + 1) * paced) // chunks, row, 0)
-        cross_copy(c).wait_recv()
-        along_copy(c).start()
-
-        @pl.when(c >= lag)
+        lax.fori_loop(upto(c), upto(c + 1), row, 0)
+        onto_next(c)
+
+        @pl.when(c == 1)
         def _():
-            along_copy(c - lag).wait_recv()
-            twin_copy(c - lag).start()
+            onto_twin(first)
+            onto_twin(first + 1)
+
+        @pl.when(c >= 2)
+        def _():
+            onto_twin(c - 2)
 
         return carry
 
-    lax.fori_loop(0, chunks, turn, 0)
-
-    def tail(i):
-        every(2, lambda j: build(paced + 2 * i + j))
-        along_copy(chunks - lag + i).wait_recv()
-        twin_copy(chunks - lag + i).start()
-
-    every(lag, tail)
+    lax.fori_loop(0, main, turn, 0)
+    onto_next(last)
+    onto_next(last + 1)
+    every(2, lambda j: build(paced + j))
+    onto_twin(main - 2)
+    every(3, lambda j: build(paced + 2 + j))
+    for c in (main - 1, last, last + 1):
+        onto_twin(c)
     own_copy().wait_recv()
     all_rows(twin_s, twin_r).wait_recv()
 
@@ -335,7 +362,6 @@
 def image_and_gram(near, ranges, coords, own, slabs, total):
     rows, size, rank = own.shape
     slots = near.shape[1]
-    chunks = 8
     late = rows // 4
     early = rows - late
     vmem = pl.BlockSpec(memory_space=pltpu.VMEM)
@@ -366,7 +392,7 @@
         + [pltpu.VMEM((n, piece, rank), F32) for n in (8, 8, 4, 8, 8)]
         + [pltpu.VMEM((piece, rank), F32)] * 3
         + [dma(())] * 2
-        + [dma(()), dma((chunks,))] * 2
+        + [dma(()), dma((10,))] * 2
         + [dma(())] * 12
         + [dma(())],
         compiler_params=pltpu.CompilerParams(

time: 106 us -> 107 us (level)
  no operation moved by 1% of the time
where the time goes in v7:
time: 107 us
  Pallas kernels  106 us (99%)
    pallas_call x1, Pallas kernels, image_and_gram(): pl.pallas_call(functools.partial(image_kernel, total, slabs), name='image...  80.3 us
    pallas_call x1, Pallas kernels, basis_and_factor(): pl.pallas_call(basis_kernel, name='basis', out_shape=(jax.ShapeDtypeStruc...  26.1 us

profile of v7, /device:TPU:1, one launch (start us, length us, event | category | flops | bytes accessed | tf_op | source)
XLA Modules:
  0.0 107.1 jit_solution(16813684927153805182)
XLA Ops:
  0.6 80.3 %image.1 = (f32[32,128,128]{2,1,0:T(8,128)}, f32[8,16,128]{2,1,0:T(8,128)}) custom-call(s32[32,32]{1,0:T(8,128)} %near.1, f32[3]{0:T(128)} %ranges.1, s32[3,4096]{1,0:T(4,128)} %coords_ref.1, bf16[32,128,128]{2,1,0:T(8,128)(2,1)} %bitcast.4), custom_call_target="tpu_custom_call" | custom-call | tf_op jit(solution)/shard_map/image/pallas_call | solution.py:371
  81.0 26.1 %basis.1 = (f32[4096,128]{1,0:T(8,128)}, f32[128,128]{1,0:T(8,128)}) custom-call(f32[128,128]{1,0:T(8,128)} %bitcast.5, f32[4096,128]{1,0:T(8,128)} %bitcast.3), custom_call_target="tpu_custom_call" | custom-call | tf_op jit(solution)/shard_map/basis/pallas_call | solution.py:511

commit v8 on v7

--- a/solution.py
+++ b/solution.py
@@ -162,7 +162,7 @@
 
     for i in range(4):
         place_copy(i).start()
-    for c in (first, first + 1, *range(main), last, last + 1):
+    for c in (first, first + 1, 0, 1):
         cross_copy(c).start()
     own_copy().start()
     wide_ref[pl.ds(2 * rows, rows)] = own_ref[...]
@@ -206,7 +206,9 @@
         twin_copy(c).start()
 
     onto_next(first)
+    cross_copy(2).start()
     onto_next(first + 1)
+    cross_copy(3).start()
     for step in (0, 1, 3, 4):
         both, norm = spread(place_ref[step], step)
         put_right(both, norm, step)
@@ -245,6 +247,18 @@
 
         lax.fori_loop(upto(c), upto(c + 1), row, 0)
         onto_next(c)
+
+        @pl.when(c < 2)
+        def _():
+            cross_copy(c + 4).start()
+
+        @pl.when(c == 2)
+        def _():
+            cross_copy(last).start()
+
+        @pl.when(c == 3)
+        def _():
+            cross_copy(last + 1).start()
 
         @pl.when(c == 1)
         def _():

time: 107 us -> 107 us (level)
  no operation moved by 1% of the time
where the time goes in v8:
time: 107 us
  Pallas kernels  106 us (99%)
    pallas_call x1, Pallas kernels, image_and_gram(): pl.pallas_call(functools.partial(image_kernel, total, slabs), name='image...  80.3 us
    pallas_call x1, Pallas kernels, basis_and_factor(): pl.pallas_call(basis_kernel, name='basis', out_shape=(jax.ShapeDtypeStruc...  26.1 us

profile of v8, /device:TPU:1, one launch (start us, length us, event | category | flops | bytes accessed | tf_op | source)
XLA Modules:
  0.0 107.1 jit_solution(7826748410255090671)
XLA Ops:
  0.6 80.3 %image.1 = (f32[32,128,128]{2,1,0:T(8,128)}, f32[8,16,128]{2,1,0:T(8,128)}) custom-call(s32[32,32]{1,0:T(8,128)} %near.1, f32[3]{0:T(128)} %ranges.1, s32[3,4096]{1,0:T(4,128)} %coords_ref.1, bf16[32,128,128]{2,1,0:T(8,128)(2,1)} %bitcast.4), custom_call_target="tpu_custom_call" | custom-call | tf_op jit(solution)/shard_map/image/pallas_call | solution.py:385
  81.0 26.1 %basis.1 = (f32[4096,128]{1,0:T(8,128)}, f32[128,128]{1,0:T(8,128)}) custom-call(f32[128,128]{1,0:T(8,128)} %bitcast.5, f32[4096,128]{1,0:T(8,128)} %bitcast.3), custom_call_target="tpu_custom_call" | custom-call | tf_op jit(solution)/shard_map/basis/pallas_call | solution.py:525
